TPU v7x, 32 devices: a whole 2x2x4 slice. The times are simulated.
32 devices in a mesh: rep: 4 (over y, x), fsdp: 8 (over z, core).
Axes of the slice: x: 2, y: 2, z: 4, core: 2. Of those that a mesh axis runs over, the one named last changes fastest.
Arguments:
- tokens: bfloat16 [64, 512, 768], P(('rep', 'fsdp')), may hold values from -6 to 6
- memory: bfloat16 [64, 1024, 768], P(('rep', 'fsdp')), may hold values from -6 to 6
- prefix_len: int32 [64], P(('rep', 'fsdp')), may hold values from 51 to 256
- bucket_table: int32 [1023], replicated, may hold values from 0 to 31
- rel_bias: bfloat16 [384], P('fsdp'), may hold values from -4 to 4
- gain_self: bfloat16 [768], P('fsdp'), may hold values from 0.5 to 1.5
- self_query: bfloat16 [768, 768], P('fsdp'), may hold values from -0.099609375 to 0.099609375
- self_key: bfloat16 [768, 768], P('fsdp'), may hold values from -0.099609375 to 0.099609375
- self_value: bfloat16 [768, 768], P('fsdp'), may hold values from -0.21875 to 0.21875
- self_out: bfloat16 [768, 768], P('fsdp'), may hold values from -0.875 to 0.875
- gain_cross: bfloat16 [768], P('fsdp'), may hold values from 0.5 to 1.5
- cross_query: bfloat16 [768, 768], P('fsdp'), may hold values from -0.099609375 to 0.099609375
- cross_key: bfloat16 [768, 768], P('fsdp'), may hold values from -0.099609375 to 0.099609375
- cross_value: bfloat16 [768, 768], P('fsdp'), may hold values from -0.21875 to 0.21875
- cross_out: bfloat16 [768, 768], P('fsdp'), may hold values from -1.25 to 1.25
- gain_feed: bfloat16 [768], P('fsdp'), may hold values from 0.5 to 1.5
- gate_weight: bfloat16 [768, 2048], P('fsdp'), may hold values from -0.21875 to 0.21875
- up_weight: bfloat16 [768, 2048], P('fsdp'), may hold values from -0.21875 to 0.21875
- down_weight: bfloat16 [2048, 768], P('fsdp'), may hold values from -0.25 to 0.25
- out_grad: bfloat16 [64, 512, 768], P(('rep', 'fsdp')), may hold values from -6 to 6
Outputs:
- layer_out: bfloat16 [64, 512, 768], P(('rep', 'fsdp'))
- tokens_grad: float32 [64, 512, 768], P(('rep', 'fsdp'))
- memory_grad: float32 [64, 1024, 768], P(('rep', 'fsdp'))
- rel_bias_grad: float32 [384], P('fsdp')
- gain_self_grad: float32 [768], P('fsdp')
- self_query_grad: float32 [768, 768], P('fsdp', 'rep')
- self_key_grad: float32 [768, 768], P('fsdp', 'rep')
- self_value_grad: float32 [768, 768], P('fsdp', 'rep')
- self_out_grad: float32 [768, 768], P('fsdp', 'rep')
- gain_cross_grad: float32 [768], P('fsdp')
- cross_query_grad: float32 [768, 768], P('fsdp', 'rep')
- cross_key_grad: float32 [768, 768], P('fsdp', 'rep')
- cross_value_grad: float32 [768, 768], P('fsdp', 'rep')
- cross_out_grad: float32 [768, 768], P('fsdp', 'rep')
- gain_feed_grad: float32 [768], P('fsdp')
- gate_weight_grad: float32 [768, 2048], P('fsdp', 'rep')
- up_weight_grad: float32 [768, 2048], P('fsdp', 'rep')
- down_weight_grad: float32 [2048, 768], P('fsdp', 'rep')
All inputs are finite; a program needn't handle non-finite values.
Results may differ from a plain program's by a relative error of at most 0.03.
Values may be sent and summed in bfloat16 or wider, within the bound.
A program may use at most 384 MiB of HBM per device.

v0:
```python
import functools

import jax
import jax.numpy as jnp
from jax import lax
from jax.sharding import PartitionSpec as P

NHEAD = 12
DHEAD = 64
BUCKETS = 32


EPSILON = 1e-06
CUBIC_TERM = 0.044715
SQRT_TWO_PI = 0.7978845608028654
NEGATIVE = -1000000000.0
PRECISE = lax.Precision.HIGHEST


def shortened(array):
    return jax.tree.map(lambda a: a.astype(jnp.bfloat16) if a.dtype == jnp.float32 else a, array)


def matmul(left_side, right_side):
    return jnp.dot(left_side, right_side, preferred_element_type=jnp.float32)


def weight_term(inputs, gradient):
    return lax.dot_general(
        inputs, gradient, (((0,), (0,)), ((), ())), preferred_element_type=jnp.float32
    )


def back_term(gradient, weight):
    return lax.dot_general(
        gradient, weight, (((1,), (1,)), ((), ())), preferred_element_type=jnp.float32
    )


def inverse_rms(values):
    return lax.rsqrt(jnp.mean(values * values, axis=-1, keepdims=True) + EPSILON)


def gelu_tanh(values):
    return (
        0.5
        * values
        * (1.0 + jnp.tanh(SQRT_TWO_PI * (values + CUBIC_TERM * values * values * values)))
    )


def gelu_slope(values):
    tangent = jnp.tanh(SQRT_TWO_PI * (values + CUBIC_TERM * values * values * values))
    return 0.5 * (1.0 + tangent) + 0.5 * values * (1.0 - tangent * tangent) * SQRT_TWO_PI * (
        1.0 + 3.0 * CUBIC_TERM * values * values
    )


def norm_back(values, scale_rows, gain_vec, upstream):
    weighted = upstream * gain_vec
    gain_grad = jnp.sum(upstream * values * scale_rows, axis=0)
    input_grad = scale_rows * weighted - values * scale_rows * scale_rows * scale_rows * jnp.mean(
        values * weighted, axis=-1, keepdims=True
    )
    return (input_grad, gain_grad)


def split_heads(values):
    return values.reshape(values.shape[0], NHEAD, DHEAD)


def position_bias(buckets, length, bias_table):
    heads_table = bias_table.reshape(NHEAD, BUCKETS)
    onehot = (buckets[:, None] == jnp.arange(BUCKETS, dtype=jnp.int32)[None, :]).astype(jnp.float32)
    by_offset = lax.dot_general(heads_table, onehot, (((1,), (1,)), ((), ())), precision=PRECISE)
    padded = jnp.concatenate([by_offset, jnp.zeros((NHEAD, 1), jnp.float32)], axis=1)
    tiled = jnp.tile(padded, (1, length))[:, : length * (2 * length - 1)]
    return tiled.reshape(NHEAD, length, 2 * length - 1)[:, :, length - 1 :]


def masked_scores(queries, key_rows, bias_terms, allowed):
    scores = jnp.einsum(
        "qhd,khd->hqk",
        split_heads(queries),
        split_heads(key_rows),
        preferred_element_type=jnp.float32,
    )
    if bias_terms is not None:
        scores = jnp.where(allowed[None], scores + bias_terms, NEGATIVE)
    return scores


def attend(queries, key_rows, value_rows, bias_terms, allowed):
    scores = masked_scores(queries, key_rows, bias_terms, allowed)
    row_top = jnp.max(scores, axis=-1, keepdims=True)
    log_total = row_top + jnp.log(jnp.sum(jnp.exp(scores - row_top), axis=-1, keepdims=True))
    shares = jnp.exp(scores - log_total).astype(jnp.bfloat16)
    context = jnp.einsum(
        "hqk,khd->qhd", shares, split_heads(value_rows), preferred_element_type=jnp.float32
    )
    return (context.reshape(queries.shape[0], -1).astype(jnp.bfloat16), log_total)


def attend_back(upstream, queries, key_rows, value_rows, bias_terms, allowed, log_total):
    scores = masked_scores(queries, key_rows, bias_terms, allowed)
    shares = jnp.exp(scores - log_total)
    heads_up = split_heads(upstream)
    value_grad = jnp.einsum(
        "hqk,qhd->khd", shares.astype(jnp.bfloat16), heads_up, preferred_element_type=jnp.float32
    )
    share_grad = jnp.einsum(
        "qhd,khd->hqk", heads_up, split_heads(value_rows), preferred_element_type=jnp.float32
    )
    row_inner = jnp.sum(shares * share_grad, axis=-1, keepdims=True)
    score_grad = (shares * (share_grad - row_inner)).astype(jnp.bfloat16)
    query_grad = jnp.einsum(
        "hqk,khd->qhd", score_grad, split_heads(key_rows), preferred_element_type=jnp.float32
    )
    key_grad = jnp.einsum(
        "hqk,qhd->khd", score_grad, split_heads(queries), preferred_element_type=jnp.float32
    )
    row_count = queries.shape[0]
    col_count = key_rows.shape[0]
    return (
        query_grad.reshape(row_count, -1).astype(jnp.bfloat16),
        key_grad.reshape(col_count, -1).astype(jnp.bfloat16),
        value_grad.reshape(col_count, -1).astype(jnp.bfloat16),
        score_grad,
    )


def forward_pass(weights, token_rows, memory_rows, bias_terms, allowed):
    (
        bias_table,
        gain_first,
        query_self,
        key_self,
        value_self,
        out_self,
        gain_second,
        query_cross,
        key_cross,
        value_cross,
        out_cross,
        gain_third,
        gate_proj,
        up_proj,
        down_proj,
    ) = weights
    start_rows = token_rows.astype(jnp.float32)
    scale_first = inverse_rms(start_rows)
    normed_first = (start_rows * scale_first * gain_first.astype(jnp.float32)).astype(jnp.bfloat16)
    queries = matmul(normed_first, query_self).astype(jnp.bfloat16)
    key_rows = matmul(normed_first, key_self).astype(jnp.bfloat16)
    value_rows = matmul(normed_first, value_self).astype(jnp.bfloat16)
    context, total_self = attend(queries, key_rows, value_rows, bias_terms, allowed)
    middle = start_rows + matmul(context, out_self)
    scale_second = inverse_rms(middle)
    normed_second = (middle * scale_second * gain_second.astype(jnp.float32)).astype(jnp.bfloat16)
    query_two = matmul(normed_second, query_cross).astype(jnp.bfloat16)
    keys_two = matmul(memory_rows, key_cross).astype(jnp.bfloat16)
    values_two = matmul(memory_rows, value_cross).astype(jnp.bfloat16)
    context_two, total_cross = attend(query_two, keys_two, values_two, None, None)
    later = middle + matmul(context_two, out_cross)
    scale_third = inverse_rms(later)
    normed_third = (later * scale_third * gain_third.astype(jnp.float32)).astype(jnp.bfloat16)
    gate_pre = matmul(normed_third, gate_proj)
    up_pre = matmul(normed_third, up_proj)
    hidden = (gelu_tanh(gate_pre) * up_pre).astype(jnp.bfloat16)
    result = (later + matmul(hidden, down_proj)).astype(jnp.bfloat16)
    saved = (
        start_rows,
        scale_first,
        normed_first,
        queries,
        key_rows,
        value_rows,
        total_self,
        context,
        middle,
        scale_second,
        normed_second,
        query_two,
        keys_two,
        values_two,
        total_cross,
        context_two,
        later,
        scale_third,
        normed_third,
        gate_pre,
        up_pre,
        hidden,
    )
    return (saved, result)


def backward_pass(weights, saved, upstream, memory_rows, bias_terms, allowed):
    (
        bias_table,
        gain_first,
        query_self,
        key_self,
        value_self,
        out_self,
        gain_second,
        query_cross,
        key_cross,
        value_cross,
        out_cross,
        gain_third,
        gate_proj,
        up_proj,
        down_proj,
    ) = weights
    (
        start_rows,
        scale_first,
        normed_first,
        queries,
        key_rows,
        value_rows,
        total_self,
        context,
        middle,
        scale_second,
        normed_second,
        query_two,
        keys_two,
        values_two,
        total_cross,
        context_two,
        later,
        scale_third,
        normed_third,
        gate_pre,
        up_pre,
        hidden,
    ) = saved
    down_grad = weight_term(hidden, upstream)
    hidden_grad = back_term(upstream, down_proj)
    gate_grad = (hidden_grad * up_pre * gelu_slope(gate_pre)).astype(jnp.bfloat16)
    lift_grad = (hidden_grad * gelu_tanh(gate_pre)).astype(jnp.bfloat16)
    gate_wgrad = weight_term(normed_third, gate_grad)
    up_wgrad = weight_term(normed_third, lift_grad)
    third_grad = back_term(gate_grad, gate_proj) + back_term(lift_grad, up_proj)
    carry_grad, gain_third_grad = norm_back(
        later, scale_third, gain_third.astype(jnp.float32), third_grad
    )
    later_grad = upstream.astype(jnp.float32) + carry_grad
    branch_two = later_grad.astype(jnp.bfloat16)
    out_cross_grad = weight_term(context_two, branch_two)
    context_two_grad = back_term(branch_two, out_cross).astype(jnp.bfloat16)
    query_two_grad, keys_two_grad, values_two_grad, cross_scores = attend_back(
        context_two_grad, query_two, keys_two, values_two, None, None, total_cross
    )
    query_cross_grad = weight_term(normed_second, query_two_grad)
    key_cross_grad = weight_term(memory_rows, keys_two_grad)
    value_cross_grad = weight_term(memory_rows, values_two_grad)
    memory_grad = back_term(keys_two_grad, key_cross) + back_term(values_two_grad, value_cross)
    carry_grad, gain_second_grad = norm_back(
        middle,
        scale_second,
        gain_second.astype(jnp.float32),
        back_term(query_two_grad, query_cross),
    )
    middle_grad = later_grad + carry_grad
    branch_one = middle_grad.astype(jnp.bfloat16)
    out_self_grad = weight_term(context, branch_one)
    context_grad = back_term(branch_one, out_self).astype(jnp.bfloat16)
    query_grad, keys_grad, values_grad, score_grad = attend_back(
        context_grad, queries, key_rows, value_rows, bias_terms, allowed, total_self
    )
    query_self_grad = weight_term(normed_first, query_grad)
    key_self_grad = weight_term(normed_first, keys_grad)
    value_self_grad = weight_term(normed_first, values_grad)
    first_grad = (
        back_term(query_grad, query_self)
        + back_term(keys_grad, key_self)
        + back_term(values_grad, value_self)
    )
    carry_grad, gain_first_grad = norm_back(
        start_rows, scale_first, gain_first.astype(jnp.float32), first_grad
    )
    start_grad = middle_grad + carry_grad
    grads = (
        gain_first_grad,
        query_self_grad,
        key_self_grad,
        value_self_grad,
        out_self_grad,
        gain_second_grad,
        query_cross_grad,
        key_cross_grad,
        value_cross_grad,
        out_cross_grad,
        gain_third_grad,
        gate_wgrad,
        up_wgrad,
        down_grad,
    )
    return (grads, score_grad, start_grad, memory_grad)


def fetch_weights(shards):
    return jax.tree.map(
        lambda part, own: part.astype(own.dtype),
        lax.all_gather(shortened(shards), "fsdp", axis=0, tiled=True),
        shards,
    )


def body(
    tokens,
    memory,
    prefix_len,
    bucket_table,
    rel_bias,
    gain_self,
    self_query,
    self_key,
    self_value,
    self_out,
    gain_cross,
    cross_query,
    cross_key,
    cross_value,
    cross_out,
    gain_feed,
    gate_weight,
    up_weight,
    down_weight,
    out_grad,
):
    shards = (
        rel_bias,
        gain_self,
        self_query,
        self_key,
        self_value,
        self_out,
        gain_cross,
        cross_query,
        cross_key,
        cross_value,
        cross_out,
        gain_feed,
        gate_weight,
        up_weight,
        down_weight,
    )
    length = tokens.shape[1]
    group_count = lax.axis_size("fsdp")
    position = jnp.arange(length, dtype=jnp.int32)
    causal = position[None, :] <= position[:, None]

    def one_micro(running, inputs):
        token_rows, memory_rows, prefix_one, grad_rows = inputs
        weights = fetch_weights(shards)
        bias_terms = position_bias(bucket_table, length, weights[0].astype(jnp.float32))
        allowed = causal | (position[None, :] < prefix_one)
        saved, result = forward_pass(weights, token_rows, memory_rows, bias_terms, allowed)
        weights = (
            lax.all_gather(shards[0], "fsdp", axis=0, tiled=True),
            lax.all_gather(shards[1], "fsdp", axis=0, tiled=True),
            lax.all_gather(shards[2], "fsdp", axis=0, tiled=True),
            lax.all_gather(shards[3], "fsdp", axis=0, tiled=True),
            lax.all_gather(shards[4], "fsdp", axis=0, tiled=True),
            lax.all_gather(shards[5], "fsdp", axis=0, tiled=True),
            lax.all_gather(shards[6], "fsdp", axis=0, tiled=True),
            lax.all_gather(shards[7], "fsdp", axis=0, tiled=True),
            lax.all_gather(shards[8], "fsdp", axis=0, tiled=True),
            lax.all_gather(shards[9], "fsdp", axis=0, tiled=True),
            lax.all_gather(shards[10], "fsdp", axis=0, tiled=True),
            lax.all_gather(shards[11], "fsdp", axis=0, tiled=True),
            lax.all_gather(shards[12], "fsdp", axis=0, tiled=True),
            lax.all_gather(shards[13], "fsdp", axis=0, tiled=True),
            lax.all_gather(shards[14], "fsdp", axis=0, tiled=True),
        )
        grads, score_grad, start_grad, memory_grad = backward_pass(
            weights, saved, grad_rows, memory_rows, bias_terms, allowed
        )
        running = (
            running[0] + score_grad.astype(jnp.float32),
            jax.tree.map(jnp.add, running[1], grads),
        )
        return (running, (result, start_grad, memory_grad))

    full_zeros = tuple(
        (
            jnp.zeros((item.shape[0] * group_count,) + item.shape[1:], jnp.float32)
            for item in shards[1:]
        )
    )
    initial = (jnp.zeros((NHEAD, length, length), jnp.float32), full_zeros)
    running, (layer_out, tokens_grad, memory_grad) = lax.scan(
        one_micro, initial, (tokens, memory, prefix_len, out_grad)
    )
    unused, pull_table = jax.vjp(
        functools.partial(position_bias, bucket_table, length),
        jnp.zeros((NHEAD * BUCKETS,), jnp.float32),
    )
    table_grad = pull_table(running[0])[0]
    owned = lax.psum_scatter((table_grad,) + running[1], "fsdp", scatter_dimension=0, tiled=True)
    vectors = lax.psum((owned[0], owned[1], owned[6], owned[11]), "rep")
    matrices = (
        lax.psum_scatter(
            owned[2].astype(jnp.bfloat16), "rep", scatter_dimension=1, tiled=True
        ).astype(jnp.float32),
        lax.psum_scatter(
            owned[3].astype(jnp.bfloat16), "rep", scatter_dimension=1, tiled=True
        ).astype(jnp.float32),
        lax.psum_scatter(
            owned[4].astype(jnp.bfloat16), "rep", scatter_dimension=1, tiled=True
        ).astype(jnp.float32),
        lax.psum_scatter(
            owned[5].astype(jnp.bfloat16), "rep", scatter_dimension=1, tiled=True
        ).astype(jnp.float32),
        lax.psum_scatter(
            owned[7].astype(jnp.bfloat16), "rep", scatter_dimension=1, tiled=True
        ).astype(jnp.float32),
        lax.psum_scatter(
            owned[8].astype(jnp.bfloat16), "rep", scatter_dimension=1, tiled=True
        ).astype(jnp.float32),
        lax.psum_scatter(
            owned[9].astype(jnp.bfloat16), "rep", scatter_dimension=1, tiled=True
        ).astype(jnp.float32),
        lax.psum_scatter(
            owned[10].astype(jnp.bfloat16), "rep", scatter_dimension=1, tiled=True
        ).astype(jnp.float32),
        lax.psum_scatter(
            owned[12].astype(jnp.bfloat16), "rep", scatter_dimension=1, tiled=True
        ).astype(jnp.float32),
        lax.psum_scatter(
            owned[13].astype(jnp.bfloat16), "rep", scatter_dimension=1, tiled=True
        ).astype(jnp.float32),
        lax.psum_scatter(
            owned[14].astype(jnp.bfloat16), "rep", scatter_dimension=1, tiled=True
        ).astype(jnp.float32),
    )
    return (
        layer_out,
        tokens_grad,
        memory_grad,
        vectors[0],
        vectors[1],
        matrices[0],
        matrices[1],
        matrices[2],
        matrices[3],
        vectors[2],
        matrices[4],
        matrices[5],
        matrices[6],
        matrices[7],
        vectors[3],
        matrices[8],
        matrices[9],
        matrices[10],
    )


def solution(mesh):
    in_specs = (
        P(("rep", "fsdp"), None, None),
        P(("rep", "fsdp"), None, None),
        P(("rep", "fsdp")),
        P(),
        P("fsdp"),
        P("fsdp"),
        P("fsdp", None),
        P("fsdp", None),
        P("fsdp", None),
        P("fsdp", None),
        P("fsdp"),
        P("fsdp", None),
        P("fsdp", None),
        P("fsdp", None),
        P("fsdp", None),
        P("fsdp"),
        P("fsdp", None),
        P("fsdp", None),
        P("fsdp", None),
        P(("rep", "fsdp"), None, None),
    )
    out_specs = (
        P(("rep", "fsdp"), None, None),
        P(("rep", "fsdp"), None, None),
        P(("rep", "fsdp"), None, None),
        P("fsdp"),
        P("fsdp"),
        P("fsdp", "rep"),
        P("fsdp", "rep"),
        P("fsdp", "rep"),
        P("fsdp", "rep"),
        P("fsdp"),
        P("fsdp", "rep"),
        P("fsdp", "rep"),
        P("fsdp", "rep"),
        P("fsdp", "rep"),
        P("fsdp"),
        P("fsdp", "rep"),
        P("fsdp", "rep"),
        P("fsdp", "rep"),
    )
    return jax.shard_map(body, mesh=mesh, in_specs=in_specs, out_specs=out_specs, check_vma=False)
```

profile of v0, /device:TPU:0, one launch (start us, length us, event | category | flops | bytes accessed | tf_op | source)
XLA Modules:
  0.0 1798.6 jit_solution(1856550587466809214)
XLA Ops:
  8.2 965.9 %while.45 = (s32[]{:T(128)}, f32[12,512,512]{1,2,0:T(8,128)}, f32[768]{0:T(1024)}, f32[768,768]{1,0:T(8,128)}, f32[768,768]{1,0:T(8,128)}, /*index=5*/f32[768,76...) while((s32[]{:T(128)}, f32[12,512,512]{1,2,0:T(8,128)}, ...), condition=%wide.region_16.17_spmd.clone, body=%wide.region_0.16_spmd.clone.sunk | while | flops 40103723008 | bytes 1790420992 | solution.py:396
  20.7 18.7 %all-reduce.19 = (bf16[768]{0:T(1024)(128)(2,1)S(1)}, bf16[384]{0:T(512)(128)(2,1)S(1)}, bf16[768]{0:T(1024)(128)(2,1)S(1)}, bf16[768]{0:T(1024)(128)(2,1)S(1)}) all-reduce(bf16[768]{0:T(1024)(128)(2,1)S(1)} %dynamic-update-slice.12, bf16[384]{0:T(512)(128)(2,1)S(1)} %dynamic-update-slice.13, ...), channel_id=1, replica_groups=mesh['rep'=4,'fsdp'=8] {'fsdp'}, use_global_device_ids=true, to_apply=%add.3 | all-reduce | flops 2688 | bytes 10752 | tf_op jit(solution)/shard_map/while
  62.7 39.9 %copy.113 = f32[2,8,512,1024]{3,1,2,0:T(8,128)} copy(f32[2,8,512,1024]{3,2,1,0:T(8,128)S(1)} %bitcast.422) | data formatting | bytes 67108864 | tf_op jit(solution)/shard_map/while
  102.6 22.9 %slice.14 = f32[12,523776]{1,0:T(8,128)} slice(f32[12,524288]{1,0:T(8,128)} %bitcast.423), slice={[0:12], [0:523776]} | slice | bytes 50282496 | tf_op jit(solution)/shard_map/while/body/eval_jaxpr/slice | solution.py:77
  125.5 54.5 %reshape.294 = f32[12,512,1023]{2,1,0:T(8,128)} reshape(f32[12,523776]{1,0:T(8,128)} %slice.14) | data formatting | bytes 50282496 | tf_op jit(solution)/shard_map/while/body/eval_jaxpr/reshape | solution.py:78
  294.3 28.0 %all-gather.32.cloned.1.call-done = bf16[768,2048]{1,0:T(8,128)(2,1)} async-done(((bf16[96,2048]{1,0:T(8,128)(2,1)}), bf16[768,2048]{1,0:T(8,128)(2,1)}) %all-gather.32.cloned.1.call-update) | async-done | bytes 3145744 | tf_op jit(solution)/shard_map/while/body/eval_jaxpr/all_gather | solution.py:308
  351.6 19.7 %multiply_reduce_fusion.17 = (f32[12,512]{1,0:T(8,128)S(1)}, f32[12,512,1024]{2,1,0:T(8,128)}) fusion(f32[12,512,1024]{2,1,0:T(8,128)} %get-tuple-element.776, f32[12,512]{1,0:T(8,128)S(1)} %log_add_fusion.5, bf16[512,12,64]{0,2,1:T(8,128)(2,1)S(1)} %bitcast.445, bf16[1024,12,64]{0,2,1:T(8,128)(2,1)S(1)} %bitcast.449), kind=kOutput, calls=%fused_computation.3.clone.1 | convolution fusion | flops 824174592 | bytes 52740096 | tf_op jit(solution)/shard_map/while/body/eval_jaxpr/qhd,khd->hqk/dot_general | solution.py:111
  541.2 39.9 %copy.113 = f32[2,8,512,1024]{3,1,2,0:T(8,128)} copy(f32[2,8,512,1024]{3,2,1,0:T(8,128)S(1)} %bitcast.422) | data formatting | bytes 67108864 | tf_op jit(solution)/shard_map/while
  581.0 22.9 %slice.14 = f32[12,523776]{1,0:T(8,128)} slice(f32[12,524288]{1,0:T(8,128)} %bitcast.423), slice={[0:12], [0:523776]} | slice | bytes 50282496 | tf_op jit(solution)/shard_map/while/body/eval_jaxpr/slice | solution.py:77
  603.9 42.0 %reshape.294 = f32[12,512,1023]{2,1,0:T(8,128)} reshape(f32[12,523776]{1,0:T(8,128)} %slice.14) | data formatting | bytes 50282496 | tf_op jit(solution)/shard_map/while/body/eval_jaxpr/reshape | solution.py:78
  767.0 33.1 %all-gather.32.cloned.1.call-done = bf16[768,2048]{1,0:T(8,128)(2,1)} async-done(((bf16[96,2048]{1,0:T(8,128)(2,1)}), bf16[768,2048]{1,0:T(8,128)(2,1)}) %all-gather.32.cloned.1.call-update) | async-done | bytes 3145744 | tf_op jit(solution)/shard_map/while/body/eval_jaxpr/all_gather | solution.py:308
  829.4 19.7 %multiply_reduce_fusion.17 = (f32[12,512]{1,0:T(8,128)S(1)}, f32[12,512,1024]{2,1,0:T(8,128)}) fusion(f32[12,512,1024]{2,1,0:T(8,128)} %get-tuple-element.776, f32[12,512]{1,0:T(8,128)S(1)} %log_add_fusion.5, bf16[512,12,64]{0,2,1:T(8,128)(2,1)S(1)} %bitcast.445, bf16[1024,12,64]{0,2,1:T(8,128)(2,1)S(1)} %bitcast.449), kind=kOutput, calls=%fused_computation.3.clone.1 | convolution fusion | flops 824174592 | bytes 52740096 | tf_op jit(solution)/shard_map/while/body/eval_jaxpr/qhd,khd->hqk/dot_general | solution.py:111
  987.4 25.3 %reduce-scatter.53.cloned.1.call-done = f32[96,768]{1,0:T(8,128)} async-done(((f32[768,768]{1,0:T(8,128)}), f32[96,768]{1,0:T(8,128)}) %reduce-scatter.53.cloned.1.call-update) | async-done | bytes 294928 | tf_op jit(solution)/shard_map/reduce_scatter | solution.py:404
  1014.6 36.2 %reduce-scatter.51.cloned.1.call-done = f32[96,768]{1,0:T(8,128)} async-done(((f32[768,768]{1,0:T(8,128)}), f32[96,768]{1,0:T(8,128)}) %reduce-scatter.51.cloned.1.call-update) | async-done | bytes 294928 | tf_op jit(solution)/shard_map/reduce_scatter | solution.py:404
  1052.6 36.1 %reduce-scatter.49.cloned.1.call-done = f32[96,768]{1,0:T(8,128)} async-done(((f32[768,768]{1,0:T(8,128)}), f32[96,768]{1,0:T(8,128)}) %reduce-scatter.49.cloned.1.call-update) | async-done | bytes 294928 | tf_op jit(solution)/shard_map/reduce_scatter | solution.py:404
  1090.6 36.3 %reduce-scatter.47.cloned.1.call-done = f32[96,768]{1,0:T(8,128)} async-done(((f32[768,768]{1,0:T(8,128)}), f32[96,768]{1,0:T(8,128)}) %reduce-scatter.47.cloned.1.call-update) | async-done | bytes 294928 | tf_op jit(solution)/shard_map/reduce_scatter | solution.py:404
  1128.8 36.3 %reduce-scatter.45.cloned.1.call-done = f32[96,768]{1,0:T(8,128)} async-done(((f32[768,768]{1,0:T(8,128)}), f32[96,768]{1,0:T(8,128)}) %reduce-scatter.45.cloned.1.call-update) | async-done | bytes 294928 | tf_op jit(solution)/shard_map/reduce_scatter | solution.py:404
  1167.0 36.3 %reduce-scatter.43.cloned.1.call-done = f32[96,768]{1,0:T(8,128)} async-done(((f32[768,768]{1,0:T(8,128)}), f32[96,768]{1,0:T(8,128)}) %reduce-scatter.43.cloned.1.call-update) | async-done | bytes 294928 | tf_op jit(solution)/shard_map/reduce_scatter | solution.py:404
  1205.1 36.1 %reduce-scatter.41.cloned.1.call-done = f32[96,768]{1,0:T(8,128)} async-done(((f32[768,768]{1,0:T(8,128)}), f32[96,768]{1,0:T(8,128)}) %reduce-scatter.41.cloned.1.call-update) | async-done | bytes 294928 | tf_op jit(solution)/shard_map/reduce_scatter | solution.py:404
  1243.1 36.1 %reduce-scatter.39.cloned.1.call-done = f32[96,768]{1,0:T(8,128)} async-done(((f32[768,768]{1,0:T(8,128)}), f32[96,768]{1,0:T(8,128)}) %reduce-scatter.39.cloned.1.call-update) | async-done | bytes 294928 | tf_op jit(solution)/shard_map/reduce_scatter | solution.py:404
  1281.1 68.8 %reduce-scatter.59.cloned.1.call-done = f32[96,2048]{1,0:T(8,128)} async-done(((f32[768,2048]{1,0:T(8,128)}), f32[96,2048]{1,0:T(8,128)}) %reduce-scatter.59.cloned.1.call-update) | async-done | bytes 786448 | tf_op jit(solution)/shard_map/reduce_scatter | solution.py:404
  1351.9 68.5 %reduce-scatter.55.cloned.1.call-done = f32[96,2048]{1,0:T(8,128)} async-done(((f32[768,2048]{1,0:T(8,128)}), f32[96,2048]{1,0:T(8,128)}) %reduce-scatter.55.cloned.1.call-update) | async-done | bytes 786448 | tf_op jit(solution)/shard_map/reduce_scatter | solution.py:404
  1452.7 38.3 %reshape.234 = f32[12,523776]{1,0:T(8,128)} reshape(f32[12,512,1023]{2,1,0:T(8,128)} %pad.7.clone) | data formatting | bytes 50282496 | tf_op jit(solution)/shard_map/transpose(jvp())/reshape | solution.py:78
  1502.9 35.9 %copy.104 = f32[2,8,512,1024]{3,2,1,0:T(8,128)} copy(f32[2,8,512,1024]{3,1,2,0:T(8,128)S(1)} %bitcast.452) | data formatting | bytes 67108864
  1550.4 26.0 %all-reduce.16 = (f32[384]{0:T(512)S(1)}, f32[768]{0:T(1024)S(1)}, f32[768]{0:T(1024)S(1)}, f32[768]{0:T(1024)S(1)}) all-reduce(f32[384]{0:T(512)S(1)} %reshape.236, f32[768]{0:T(1024)S(1)} %copy-done.70, f32[768]{0:T(1024)S(1)} %copy-done.67, f32[768]{0:T(1024)S(1)} %copy-done.64), channel_id=2, replica_groups=mesh['rep'=4,'fsdp'=8] {'fsdp'}, use_global_device_ids=true, to_apply=%region_18.19.clone | all-reduce | flops 2688 | bytes 21504
  1598.8 25.5 %reduce-scatter.73.cloned.1.call-done = bf16[192,96]{1,0:T(8,128)(2,1)} async-done(((bf16[768,96]{1,0:T(8,128)(2,1)}), bf16[192,96]{1,0:T(8,128)(2,1)}) %reduce-scatter.73.cloned.1.call-update) | async-done | bytes 36880
  1625.8 26.1 %reduce-scatter.71.cloned.1.call-done = bf16[192,96]{1,0:T(8,128)(2,1)} async-done(((bf16[768,96]{1,0:T(8,128)(2,1)}), bf16[192,96]{1,0:T(8,128)(2,1)}) %reduce-scatter.71.cloned.1.call-update) | async-done | bytes 36880
  1653.5 26.1 %reduce-scatter.69.cloned.1.call-done = bf16[192,96]{1,0:T(8,128)(2,1)} async-done(((bf16[768,96]{1,0:T(8,128)(2,1)}), bf16[192,96]{1,0:T(8,128)(2,1)}) %reduce-scatter.69.cloned.1.call-update) | async-done | bytes 36880
  1681.1 25.9 %reduce-scatter.67.cloned.1.call-done = bf16[192,96]{1,0:T(8,128)(2,1)} async-done(((bf16[768,96]{1,0:T(8,128)(2,1)}), bf16[192,96]{1,0:T(8,128)(2,1)}) %reduce-scatter.67.cloned.1.call-update) | async-done | bytes 36880
  1708.6 26.0 %reduce-scatter.61.cloned.1.call-done = bf16[96,512]{1,0:T(8,128)(2,1)} async-done(((bf16[96,2048]{1,0:T(8,128)(2,1)}), bf16[96,512]{1,0:T(8,128)(2,1)}) %reduce-scatter.61.cloned.1.call-update) | async-done | bytes 98320 | tf_op jit(solution)/shard_map/reduce_scatter | solution.py:434
  1736.1 25.8 %reduce-scatter.57.cloned.1.call-done = bf16[96,512]{1,0:T(8,128)(2,1)} async-done(((bf16[96,2048]{1,0:T(8,128)(2,1)}), bf16[96,512]{1,0:T(8,128)(2,1)}) %reduce-scatter.57.cloned.1.call-update) | async-done | bytes 98320 | tf_op jit(solution)/shard_map/reduce_scatter | solution.py:431
  1763.5 25.8 %reduce-scatter.65.cloned.1.call-done = bf16[256,192]{0,1:T(8,128)(2,1)} async-done(((bf16[256,768]{0,1:T(8,128)(2,1)}), bf16[256,192]{0,1:T(8,128)(2,1)}) %reduce-scatter.65.cloned.1.call-update) | async-done | bytes 98320 | tf_op jit(solution)/shard_map/reduce_scatter | solution.py:437
  (789 shorter events, 733.2 us)
Async XLA Ops:
  11.0 221.7 %all-gather.16.cloned.1.call-start = ((), (), s32[]{:S(2)}) async-start(), calls=%async_computation.46 | async-start | bytes 1327104 | tf_op jit(solution)/shard_map/while/body/eval_jaxpr/all_gather | solution.py:308
  11.5 223.6 %all-gather.22.cloned.1.call-start = ((), (), s32[]{:S(2)}) async-start(), calls=%async_computation.49 | async-start | bytes 1327104 | tf_op jit(solution)/shard_map/while/body/eval_jaxpr/all_gather | solution.py:308
  12.1 226.1 %all-gather.24.cloned.1.call-start = ((), (), s32[]{:S(2)}) async-start(), calls=%async_computation.50 | async-start | bytes 1327104 | tf_op jit(solution)/shard_map/while/body/eval_jaxpr/all_gather | solution.py:308
  12.7 250.6 %all-gather.20.cloned.1.call-start = ((), (), s32[]{:S(2)}) async-start(), calls=%async_computation.48 | async-start | bytes 1327104 | tf_op jit(solution)/shard_map/while/body/eval_jaxpr/all_gather | solution.py:308
  13.5 265.9 %all-gather.26.cloned.1.call-start = ((), (), s32[]{:S(2)}) async-start(), calls=%async_computation.51 | async-start | bytes 1327104 | tf_op jit(solution)/shard_map/while/body/eval_jaxpr/all_gather | solution.py:308
  14.2 267.8 %all-gather.30.cloned.1.call-start = ((), (), s32[]{:S(2)}) async-start(), calls=%async_computation.53 | async-start | bytes 3538944 | tf_op jit(solution)/shard_map/while/body/eval_jaxpr/all_gather | solution.py:378
  14.9 273.6 %all-gather.28.cloned.1.call-start = ((), (), s32[]{:S(2)}) async-start(), calls=%async_computation.52 | async-start | bytes 3538944 | tf_op jit(solution)/shard_map/while/body/eval_jaxpr/all_gather | solution.py:308
  15.5 306.7 %all-gather.32.cloned.1.call-start = ((), (), s32[]{:S(2)}) async-start(), calls=%async_computation.54 | async-start | bytes 3538944 | tf_op jit(solution)/shard_map/while/body/eval_jaxpr/all_gather | solution.py:308
  493.5 207.6 %all-gather.22.cloned.1.call-start = ((), (), s32[]{:S(2)}) async-start(), calls=%async_computation.49 | async-start | bytes 1327104 | tf_op jit(solution)/shard_map/while/body/eval_jaxpr/all_gather | solution.py:308
  494.1 210.0 %all-gather.24.cloned.1.call-start = ((), (), s32[]{:S(2)}) async-start(), calls=%async_computation.50 | async-start | bytes 1327104 | tf_op jit(solution)/shard_map/while/body/eval_jaxpr/all_gather | solution.py:308
  494.7 234.2 %all-gather.20.cloned.1.call-start = ((), (), s32[]{:S(2)}) async-start(), calls=%async_computation.48 | async-start | bytes 1327104 | tf_op jit(solution)/shard_map/while/body/eval_jaxpr/all_gather | solution.py:308
  495.2 249.7 %all-gather.26.cloned.1.call-start = ((), (), s32[]{:S(2)}) async-start(), calls=%async_computation.51 | async-start | bytes 1327104 | tf_op jit(solution)/shard_map/while/body/eval_jaxpr/all_gather | solution.py:308
  496.0 251.6 %all-gather.30.cloned.1.call-start = ((), (), s32[]{:S(2)}) async-start(), calls=%async_computation.53 | async-start | bytes 3538944 | tf_op jit(solution)/shard_map/while/body/eval_jaxpr/all_gather | solution.py:378
  496.6 264.7 %all-gather.28.cloned.1.call-start = ((), (), s32[]{:S(2)}) async-start(), calls=%async_computation.52 | async-start | bytes 3538944 | tf_op jit(solution)/shard_map/while/body/eval_jaxpr/all_gather | solution.py:308
  497.3 302.7 %all-gather.32.cloned.1.call-start = ((), (), s32[]{:S(2)}) async-start(), calls=%async_computation.54 | async-start | bytes 3538944 | tf_op jit(solution)/shard_map/while/body/eval_jaxpr/all_gather | solution.py:308
  977.3 225.9 %reduce-scatter.43.cloned.1.call-start = ((), (), s32[]{:S(2)}) async-start(), calls=%async_computation.24 | async-start | bytes 2654208 | tf_op jit(solution)/shard_map/reduce_scatter | solution.py:404
  978.0 263.1 %reduce-scatter.41.cloned.1.call-start = ((), (), s32[]{:S(2)}) async-start(), calls=%async_computation.23 | async-start | bytes 2654208 | tf_op jit(solution)/shard_map/reduce_scatter | solution.py:404
  978.6 300.6 %reduce-scatter.39.cloned.1.call-start = ((), (), s32[]{:S(2)}) async-start(), calls=%async_computation.22 | async-start | bytes 2654208 | tf_op jit(solution)/shard_map/reduce_scatter | solution.py:404
  979.2 370.7 %reduce-scatter.59.cloned.1.call-start = ((), (), s32[]{:S(2)}) async-start(), calls=%async_computation.32 | async-start | bytes 7077888 | tf_op jit(solution)/shard_map/reduce_scatter | solution.py:404
  979.8 440.5 %reduce-scatter.55.cloned.1.call-start = ((), (), s32[]{:S(2)}) async-start(), calls=%async_computation.30 | async-start | bytes 7077888 | tf_op jit(solution)/shard_map/reduce_scatter | solution.py:404
  980.6 558.3 %reduce-scatter.63.cloned.1.call-start = ((), (), s32[]{:S(2)}) async-start(), calls=%async_computation.34 | async-start | bytes 7077888 | tf_op jit(solution)/shard_map/reduce_scatter | solution.py:404
  987.4 599.8 %reduce-scatter.81.cloned.1.call-start = ((), (), s32[]{:S(2)}) async-start(), calls=%async_computation.43 | async-start | bytes 245760
  1014.5 574.2 %reduce-scatter.79.cloned.1.call-start = ((), (), s32[]{:S(2)}) async-start(), calls=%async_computation.42 | async-start | bytes 245760
  1052.5 537.7 %reduce-scatter.77.cloned.1.call-start = ((), (), s32[]{:S(2)}) async-start(), calls=%async_computation.41 | async-start | bytes 245760
  1090.6 506.7 %reduce-scatter.75.cloned.1.call-start = ((), (), s32[]{:S(2)}) async-start(), calls=%async_computation.40 | async-start | bytes 245760
  1128.8 495.5 %reduce-scatter.73.cloned.1.call-start = ((), (), s32[]{:S(2)}) async-start(), calls=%async_computation.39 | async-start | bytes 245760
  1166.9 485.0 %reduce-scatter.71.cloned.1.call-start = ((), (), s32[]{:S(2)}) async-start(), calls=%async_computation.38 | async-start | bytes 245760
  1205.0 474.5 %reduce-scatter.69.cloned.1.call-start = ((), (), s32[]{:S(2)}) async-start(), calls=%async_computation.37 | async-start | bytes 245760
  1243.0 464.0 %reduce-scatter.67.cloned.1.call-start = ((), (), s32[]{:S(2)}) async-start(), calls=%async_computation.36 | async-start | bytes 245760
  1281.0 453.5 %reduce-scatter.61.cloned.1.call-start = ((), (), s32[]{:S(2)}) async-start(), calls=%async_computation.33 | async-start | bytes 491520 | tf_op jit(solution)/shard_map/reduce_scatter | solution.py:434
  1351.8 410.1 %reduce-scatter.57.cloned.1.call-start = ((), (), s32[]{:S(2)}) async-start(), calls=%async_computation.31 | async-start | bytes 491520 | tf_op jit(solution)/shard_map/reduce_scatter | solution.py:431
  1422.3 367.0 %reduce-scatter.65.cloned.1.call-start = ((), (), s32[]{:S(2)}) async-start(), calls=%async_computation.35 | async-start | bytes 491520 | tf_op jit(solution)/shard_map/reduce_scatter | solution.py:437
  (219 other events, 4004.5 us)
Sparse Core Ops, SparseCore 0:
  11.2 25.8 all-gather.17
  38.7 22.3 all-gather.13
  62.7 22.4 all-gather.11
  86.7 22.4 all-gather.15
  110.6 22.4 all-gather.21
  134.6 22.4 all-gather.23
  158.7 22.4 all-gather.19
  182.8 22.4 all-gather.25
  206.9 37.8 all-gather.29
  246.3 37.1 all-gather.27
  285.1 37.1 all-gather.31
  493.1 21.9 all-gather.17
  516.8 22.4 all-gather.13
  540.7 22.4 all-gather.11
  564.7 22.4 all-gather.15
  588.6 22.4 all-gather.21
  612.6 22.4 all-gather.23
  636.5 22.4 all-gather.19
  660.6 22.4 all-gather.25
  684.6 37.8 all-gather.29
  724.1 37.1 all-gather.27
  762.9 37.1 all-gather.31
Sparse Core Ops, SparseCore 1:
  976.9 35.8 reduce-scatter.52
  1014.9 35.8 reduce-scatter.50
  1052.9 35.8 reduce-scatter.48
  1091.1 35.8 reduce-scatter.46
  1129.3 35.8 reduce-scatter.44
  1167.4 35.7 reduce-scatter.42
  1205.4 35.7 reduce-scatter.40
  1243.4 35.8 reduce-scatter.38
  1281.4 68.4 reduce-scatter.58
  1352.2 68.1 reduce-scatter.54
  1422.5 68.1 reduce-scatter.62
  1493.5 22.7 reduce-scatter.80
  1518.9 24.2 reduce-scatter.78
  1545.9 24.2 reduce-scatter.76
  1573.0 24.2 reduce-scatter.74
  1600.0 24.2 reduce-scatter.72
  1627.7 24.2 reduce-scatter.70
  1655.3 24.2 reduce-scatter.68
  1682.7 24.2 reduce-scatter.66
  1709.8 24.7 reduce-scatter.60
  1737.2 24.6 reduce-scatter.56
  1764.6 24.7 reduce-scatter.64
where the time goes:
time: 1800 us
  waiting for transfers between devices  690 us (38%)
  local copies, waits for them, and re-layouts  527 us (29%)
  matrix products  355 us (20%)
  other arithmetic  127 us (7%)
  blocking collectives  70.5 us (4%)
    reduce_scatter x11, waiting for transfers between devices, body(): lax.psum_scatter((table_grad,) + running[1], 'fsdp', scatter_dimension=0,...  416 us
    while x428, local copies, waits for them, and re-layouts  187 us
    reshape x3, local copies, waits for them, and re-layouts, position_bias(): return tiled.reshape(NHEAD, length, 2 * length - 1)[:, :, length - 1:]  135 us
    unnamed x30, waiting for transfers between devices  115 us
    dot_general x22, matrix products, matmul(): return jnp.dot(left_side, right_side, preferred_element_type=jnp.float32)  79.5 us
    all_gather x20, waiting for transfers between devices, fetch_weights(): lax.all_gather(shortened(shards), 'fsdp', axis=0, tiled=True)  68.4 us
    unnamed x33, local copies, waits for them, and re-layouts  63.3 us
    dot_general x4, matrix products, attend_back(): jnp.einsum('qhd,khd->hqk', heads_up, split_heads(value_rows), preferred_e...  57.3 us
  transfers between devices with their start and end apart: 44, of which 21 were waited for; matrix products, arithmetic and copies ran while one was open for 37% of the time, Pallas kernels for 0%

commit v1 on v0

v1 whole, which is shorter than its diff:
```python
import functools

import jax
import jax.numpy as jnp
from jax import lax
from jax.experimental import pallas as pl
from jax.experimental.pallas import tpu as pltpu
from jax.sharding import PartitionSpec as P

NHEAD = 12
DHEAD = 64
BUCKETS = 32
PAIRS = NHEAD // 2
LANES = 2 * DHEAD
PREFIX_MAX = 256

EPSILON = 1e-06
CUBIC_TERM = 0.044715
SQRT_TWO_PI = 0.7978845608028654
NEGATIVE = -1000000000.0

F32 = jnp.float32
BF16 = jnp.bfloat16
LAST_DIMS = (((1,), (1,)), ((), ()))
FIRST_DIMS = (((0,), (0,)), ((), ()))


def matmul(left_side, right_side):
    return jnp.dot(left_side, right_side, preferred_element_type=F32)


def weight_term(inputs, gradient):
    return lax.dot_general(inputs, gradient, FIRST_DIMS, preferred_element_type=F32)


def back_term(gradient, weight):
    return lax.dot_general(gradient, weight, LAST_DIMS, preferred_element_type=F32)


def inverse_rms(values):
    return lax.rsqrt(jnp.mean(values * values, axis=-1, keepdims=True) + EPSILON)


def gelu_tanh(values):
    return (
        0.5
        * values
        * (1.0 + jnp.tanh(SQRT_TWO_PI * (values + CUBIC_TERM * values * values * values)))
    )


def gelu_slope(values):
    tangent = jnp.tanh(SQRT_TWO_PI * (values + CUBIC_TERM * values * values * values))
    return 0.5 * (1.0 + tangent) + 0.5 * values * (1.0 - tangent * tangent) * SQRT_TWO_PI * (
        1.0 + 3.0 * CUBIC_TERM * values * values
    )


def norm_back(values, scale_rows, gain_vec, upstream):
    weighted = upstream * gain_vec
    gain_grad = jnp.sum(upstream * values * scale_rows, axis=0)
    input_grad = scale_rows * weighted - values * scale_rows * scale_rows * scale_rows * jnp.mean(
        values * weighted, axis=-1, keepdims=True
    )
    return (input_grad, gain_grad)


def one_head(rows, head):
    lane = lax.broadcasted_iota(jnp.int32, rows.shape, 1)
    keep = lane < DHEAD if head == 0 else lane >= DHEAD
    return jnp.where(keep, rows, jnp.zeros_like(rows))


def flipped(rows):
    return rows.astype(F32).T.astype(BF16)


def tree(fold, rows, groups):
    step = rows.shape[0] // groups
    total = rows[:step]
    for index in range(1, groups):
        total = fold(total, rows[index * step : (index + 1) * step])
    return total


def column_max(rows, groups):
    return jnp.max(tree(jnp.maximum, rows, groups), axis=0, keepdims=True)


def column_sum(rows, groups):
    return jnp.sum(tree(jnp.add, rows, groups), axis=0, keepdims=True)


def allowed_at(shape, key_start, query_start, prefix):
    key = lax.broadcasted_iota(jnp.int32, shape, 0) + key_start
    query = lax.broadcasted_iota(jnp.int32, shape, 1) + query_start
    return (key <= query) | (key < prefix)


def skew_kernel(table_ref, buckets_ref, out_ref):
    bucket = lax.broadcasted_iota(jnp.int32, (BUCKETS, buckets_ref.shape[1]), 0)
    onehot = (bucket == buckets_ref[...]).astype(BF16)
    by_offset = matmul(table_ref[...], onehot)
    width = out_ref.shape[2]
    total = by_offset.shape[1]
    for head in range(NHEAD):
        rows = jnp.broadcast_to(by_offset[head : head + 1], (LANES, total))
        rolled = pltpu.roll(rows, total - (LANES - 1), 1, stride=1, stride_axis=0)
        out_ref[head] = rolled[:, :width]


def skewed_bias(table, buckets_back, length):
    total = 2 * length
    return pl.pallas_call(
        skew_kernel,
        out_shape=jax.ShapeDtypeStruct((NHEAD, LANES, total - LANES), F32),
        name="skewed_bias",
    )(jnp.pad(table, ((0, 4), (0, 0))), buckets_back)


def self_forward(prefix_ref, qkv_ref, bias_ref, out_ref, lse_ref):
    length = qkv_ref.shape[0]
    block = 256
    prefix = prefix_ref[pl.program_id(0)]
    queries = qkv_ref[:, :LANES]
    keys = qkv_ref[:, LANES : 2 * LANES]
    values = flipped(qkv_ref[:, 2 * LANES :])
    for start in range(0, length, block):
        stop = start + block
        count = max(PREFIX_MAX, stop)
        outs = []
        for head in range(2):
            scores = back_term(keys[:count], one_head(queries[start:stop], head))
            parts = []
            for base in range(0, count, LANES):
                shift = length - LANES - base + start
                part = scores[base : base + LANES] + bias_ref[head, :, shift : shift + block]
                if base + LANES - 1 > start:
                    part = jnp.where(
                        allowed_at(part.shape, base, start, prefix), part, NEGATIVE
                    )
                parts.append(part)
            top = parts[0]
            for part in parts[1:]:
                top = jnp.maximum(top, part)
            top = column_max(top, 4)
            shares = [jnp.exp(part - top) for part in parts]
            total = shares[0]
            for share in shares[1:]:
                total = total + share
            total = column_sum(total, 4)
            share = jnp.concatenate([item.astype(BF16) for item in shares], axis=0)
            context = matmul(values[head * DHEAD : (head + 1) * DHEAD, :count], share)
            outs.append(context * (1.0 / total))
            lse_ref[head : head + 1, start:stop] = top + jnp.log(total)
        out_ref[start:stop, :] = jnp.concatenate(outs, axis=0).T.astype(BF16)


def cross_forward(query_ref, kv_ref, out_ref, lse_ref):
    length = query_ref.shape[0]
    keys = kv_ref[:, :LANES]
    values = flipped(kv_ref[:, LANES:])
    queries = query_ref[...]
    ahead = [back_term(keys, one_head(queries, head)) for head in range(2)]
    outs = []
    for head in range(2):
        scores = ahead[head]
        top = column_max(scores, 16)
        share = jnp.exp(scores - top)
        total = column_sum(share, 16)
        context = matmul(values[head * DHEAD : (head + 1) * DHEAD], share.astype(BF16))
        outs.append(context * (1.0 / total))
        lse_ref[head : head + 1, :] = top + jnp.log(total)
    out_ref[...] = jnp.concatenate(outs, axis=0).T.astype(BF16)


def cross_backward(query_ref, kv_ref, up_ref, context_ref, lse_ref, dq_ref, dkv_ref):
    length = query_ref.shape[0]
    block = 256
    keys = kv_ref[:, :LANES]
    values = kv_ref[:, LANES:]
    queries = query_ref[...]
    upstream = up_ref[...]
    keys_flipped = flipped(keys)
    inner = (upstream.astype(F32) * context_ref[...].astype(F32)).T
    key_grad = None
    value_grad = None
    for start in range(0, length, block):
        rows = slice(start, start + block)
        grads = []
        for head in range(2):
            sub = slice(head * DHEAD, (head + 1) * DHEAD)
            query = one_head(queries[rows], head)
            above = one_head(upstream[rows], head)
            row_inner = jnp.sum(inner[sub, rows], axis=0, keepdims=True)
            shares = jnp.exp(back_term(keys, query) - lse_ref[head : head + 1, rows])
            share_grad = back_term(values, above)
            score_grad = (shares * (share_grad - row_inner)).astype(BF16)
            value_part = matmul(shares.astype(BF16), above)
            key_part = matmul(score_grad, query)
            value_grad = value_part if value_grad is None else value_grad + value_part
            key_grad = key_part if key_grad is None else key_grad + key_part
            grads.append(matmul(keys_flipped[sub], score_grad))
        dq_ref[rows, :] = jnp.concatenate(grads, axis=0).T.astype(BF16)
    dkv_ref[:, :LANES] = key_grad.astype(BF16)
    dkv_ref[:, LANES:] = value_grad.astype(BF16)


def self_backward(
    prefix_ref, qkv_ref, up_ref, context_ref, lse_ref, bias_ref, grad_ref, diag_ref, acc_ref
):
    length = qkv_ref.shape[0]
    block = 256
    step = pl.program_id(1)
    prefix = prefix_ref[step]

    @pl.when(step == 0)
    def _():
        acc_ref[...] = jnp.zeros_like(acc_ref)

    queries = qkv_ref[:, :LANES]
    keys = qkv_ref[:, LANES : 2 * LANES]
    values = qkv_ref[:, 2 * LANES :]
    upstream = up_ref[...]
    keys_flipped = flipped(keys)
    inner = (upstream.astype(F32) * context_ref[...].astype(F32)).T
    count_all = length // block
    key_grad = [None] * count_all
    value_grad = [None] * count_all
    for start in range(0, length, block):
        stop = start + block
        count = max(PREFIX_MAX, stop)
        rows = slice(start, stop)
        grads = []
        for head in range(2):
            sub = slice(head * DHEAD, (head + 1) * DHEAD)
            query = one_head(queries[rows], head)
            above = one_head(upstream[rows], head)
            row_inner = jnp.sum(inner[sub, rows], axis=0, keepdims=True)
            row_lse = lse_ref[head : head + 1, rows]
            scores = back_term(keys[:count], query)
            share_grad = back_term(values[:count], above)
            shares = []
            score_grads = []
            for base in range(0, count, LANES):
                part = slice(base, base + LANES)
                shift = length - LANES - base + start
                share = jnp.exp(
                    scores[part] + bias_ref[head, :, shift : shift + block] - row_lse
                )
                if base + LANES - 1 > start:
                    share = jnp.where(allowed_at(share.shape, base, start, prefix), share, 0.0)
                score_grad = share * (share_grad[part] - row_inner)
                acc_ref[head, :, shift : shift + block] += score_grad
                shares.append(share.astype(BF16))
                score_grads.append(score_grad.astype(BF16))
            share = jnp.concatenate(shares, axis=0)
            score_grad = jnp.concatenate(score_grads, axis=0)
            value_part = matmul(share, above)
            key_part = matmul(score_grad, query)
            for index in range(count // block):
                part = slice(index * block, (index + 1) * block)
                if value_grad[index] is None:
                    value_grad[index] = value_part[part]
                    key_grad[index] = key_part[part]
                else:
                    value_grad[index] = value_grad[index] + value_part[part]
                    key_grad[index] = key_grad[index] + key_part[part]
            grads.append(matmul(keys_flipped[sub, :count], score_grad))
        grad_ref[rows, :LANES] = jnp.concatenate(grads, axis=0).T.astype(BF16)
    for index in range(count_all):
        part = slice(index * block, (index + 1) * block)
        grad_ref[part, LANES : 2 * LANES] = key_grad[index].astype(BF16)
        grad_ref[part, 2 * LANES :] = value_grad[index].astype(BF16)

    @pl.when(step == pl.num_programs(1) - 1)
    def _():
        row = lax.broadcasted_iota(jnp.int32, (LANES, 2 * length), 0)
        amount = LANES - 1 - row
        for head in range(2):
            skewed = jnp.concatenate(
                [acc_ref[head], jnp.zeros((LANES, LANES), F32)], axis=1
            )
            bit = 1
            while bit < LANES:
                skewed = jnp.where((amount & bit) != 0, pltpu.roll(skewed, bit, 1), skewed)
                bit *= 2
            diag_ref[head : head + 1, :] = jnp.sum(skewed, axis=0, keepdims=True)


def spec(shape, index):
    return pl.BlockSpec(shape, index)


def run_self_forward(prefix, qkv, bias, nseq):
    length = qkv.shape[0] // nseq
    return pl.pallas_call(
        self_forward,
        grid_spec=pltpu.PrefetchScalarGridSpec(
            num_scalar_prefetch=1,
            grid=(nseq, PAIRS),
            in_specs=[
                spec((length, 3 * LANES), lambda s, p, _: (s, p)),
                spec((2, LANES, 2 * length - LANES), lambda s, p, _: (p, 0, 0)),
            ],
            out_specs=[
                spec((length, LANES), lambda s, p, _: (s, p)),
                spec((None, None, 2, length), lambda s, p, _: (s, p, 0, 0)),
            ],
        ),
        out_shape=[
            jax.ShapeDtypeStruct((qkv.shape[0], PAIRS * LANES), BF16),
            jax.ShapeDtypeStruct((nseq, PAIRS, 2, length), F32),
        ],
        cost_estimate=pl.CostEstimate(
            flops=20_000_000_000, bytes_accessed=12_000_000, transcendentals=0
        ),
        name="self_forward",
    )(prefix, qkv, bias)


def run_cross_forward(query, kv, nseq):
    length = query.shape[0] // nseq
    count = kv.shape[0] // nseq
    return pl.pallas_call(
        cross_forward,
        grid=(nseq, PAIRS),
        in_specs=[
            spec((length, LANES), lambda s, p: (s, p)),
            spec((count, 2 * LANES), lambda s, p: (s, p)),
        ],
        out_specs=[
            spec((length, LANES), lambda s, p: (s, p)),
            spec((None, None, 2, length), lambda s, p: (s, p, 0, 0)),
        ],
        out_shape=[
            jax.ShapeDtypeStruct(query.shape, BF16),
            jax.ShapeDtypeStruct((nseq, PAIRS, 2, length), F32),
        ],
        cost_estimate=pl.CostEstimate(
            flops=24_000_000_000, bytes_accessed=10_000_000, transcendentals=0
        ),
        name="cross_forward",
    )(query, kv)


def run_cross_backward(query, kv, upstream, context, lse, nseq):
    length = query.shape[0] // nseq
    count = kv.shape[0] // nseq
    rows = spec((length, LANES), lambda s, p: (s, p))
    wide = spec((count, 2 * LANES), lambda s, p: (s, p))
    return pl.pallas_call(
        cross_backward,
        grid=(nseq, PAIRS),
        in_specs=[
            rows,
            wide,
            rows,
            rows,
            spec((None, None, 2, length), lambda s, p: (s, p, 0, 0)),
        ],
        out_specs=[rows, wide],
        out_shape=[
            jax.ShapeDtypeStruct(query.shape, BF16),
            jax.ShapeDtypeStruct(kv.shape, BF16),
        ],
        cost_estimate=pl.CostEstimate(
            flops=36_000_000_000, bytes_accessed=20_000_000, transcendentals=0
        ),
        name="cross_backward",
    )(query, kv, upstream, context, lse)


def run_self_backward(prefix, qkv, upstream, context, lse, bias, nseq):
    length = qkv.shape[0] // nseq
    rows = spec((length, LANES), lambda p, s, _: (s, p))
    wide = spec((length, 3 * LANES), lambda p, s, _: (s, p))
    return pl.pallas_call(
        self_backward,
        grid_spec=pltpu.PrefetchScalarGridSpec(
            num_scalar_prefetch=1,
            grid=(PAIRS, nseq),
            in_specs=[
                wide,
                rows,
                rows,
                spec((None, None, 2, length), lambda p, s, _: (s, p, 0, 0)),
                spec((2, LANES, 2 * length - LANES), lambda p, s, _: (p, 0, 0)),
            ],
            out_specs=[
                wide,
                spec((None, 2, 2 * length), lambda p, s, _: (p, 0, 0)),
            ],
            scratch_shapes=[pltpu.VMEM((2, LANES, 2 * length - LANES), F32)],
        ),
        out_shape=[
            jax.ShapeDtypeStruct(qkv.shape, BF16),
            jax.ShapeDtypeStruct((PAIRS, 2, 2 * length), F32),
        ],
        cost_estimate=pl.CostEstimate(
            flops=24_000_000_000, bytes_accessed=20_000_000, transcendentals=0
        ),
        name="self_backward",
    )(prefix, qkv, upstream, context, lse, bias)


def interleave(*parts):
    blocks = []
    for pair in range(PAIRS):
        for part in parts:
            blocks.append(part[:, pair * LANES : (pair + 1) * LANES])
    return jnp.concatenate(blocks, axis=1)


def deinterleave(block, count):
    rows = block.shape[0]
    split = block.reshape(rows, PAIRS, count, LANES)
    return [split[:, :, index].reshape(rows, PAIRS * LANES) for index in range(count)]


def gather(block):
    return lax.all_gather(block, "fsdp", axis=0, tiled=True)


def scatter(block):
    return lax.psum_scatter(block.astype(BF16), "fsdp", scatter_dimension=0, tiled=True)


def scatter_columns(parts):
    count = lax.axis_size("rep")
    rows = parts[0].shape[0]
    split = [part.reshape(rows, count, -1) for part in parts]
    joined = jnp.concatenate(split, axis=2).reshape(rows, -1)
    own = lax.psum_scatter(joined, "rep", scatter_dimension=1, tiled=True)
    sizes = [part.shape[1] // count for part in parts]
    outs = []
    start = 0
    for size in sizes:
        outs.append(own[:, start : start + size].astype(F32))
        start += size
    return outs


def body(
    tokens,
    memory,
    prefix_len,
    bucket_table,
    rel_bias,
    gain_self,
    self_query,
    self_key,
    self_value,
    self_out,
    gain_cross,
    cross_query,
    cross_key,
    cross_value,
    cross_out,
    gain_feed,
    gate_weight,
    up_weight,
    down_weight,
    out_grad,
):
    nseq, length, width = tokens.shape
    shard = gain_self.shape[0]
    groups = width // shard
    entries = rel_bias.shape[0]
    small = jnp.stack(
        [gain_self, gain_cross, gain_feed, jnp.pad(rel_bias, (0, shard - entries))], axis=1
    )
    small = jnp.pad(small, ((0, 0), (0, LANES - 4)))
    first = gather(
        jnp.concatenate([interleave(self_query, self_key, self_value), small], axis=1)
    )
    second = gather(
        jnp.concatenate(
            [self_out, cross_query, interleave(cross_key, cross_value), cross_out], axis=1
        )
    )
    gate_up = gather(jnp.concatenate([gate_weight, up_weight], axis=1))
    down = gather(down_weight)
    qkv_proj = first[:, : 3 * width]
    vectors = first[:, 3 * width : 3 * width + 4].T
    gain_first = vectors[0:1].astype(F32)
    gain_second = vectors[1:2].astype(F32)
    gain_third = vectors[2:3].astype(F32)
    table = vectors[3].reshape(groups, shard)[:, :entries].reshape(NHEAD, BUCKETS)
    out_self = second[:, :width]
    query_cross = second[:, width : 2 * width]
    kv_cross = second[:, 2 * width : 4 * width]
    out_cross = second[:, 4 * width :]
    ffn = gate_weight.shape[1]
    gate_proj = gate_up[:, :ffn]
    up_proj = gate_up[:, ffn:]

    buckets_back = jnp.pad(bucket_table[::-1], (0, 1)).reshape(1, 2 * length)
    bias = skewed_bias(table, buckets_back, length)

    rows = nseq * length
    start_rows = tokens.reshape(rows, width).astype(F32)
    memory_rows = memory.reshape(-1, width)
    upstream = out_grad.reshape(rows, width)

    scale_first = inverse_rms(start_rows)
    normed_first = (start_rows * scale_first * gain_first).astype(BF16)
    qkv = matmul(normed_first, qkv_proj).astype(BF16)
    context, lse_self = run_self_forward(prefix_len, qkv, bias, nseq)
    middle = start_rows + matmul(context, out_self)
    scale_second = inverse_rms(middle)
    normed_second = (middle * scale_second * gain_second).astype(BF16)
    query_two = matmul(normed_second, query_cross).astype(BF16)
    kv_two = matmul(memory_rows, kv_cross).astype(BF16)
    context_two, lse_cross = run_cross_forward(query_two, kv_two, nseq)
    later = middle + matmul(context_two, out_cross)
    scale_third = inverse_rms(later)
    normed_third = (later * scale_third * gain_third).astype(BF16)
    gate_pre = matmul(normed_third, gate_proj)
    up_pre = matmul(normed_third, up_proj)
    hidden = (gelu_tanh(gate_pre) * up_pre).astype(BF16)
    result = (later + matmul(hidden, down)).astype(BF16)

    down_own = scatter(weight_term(hidden, upstream))
    hidden_grad = back_term(upstream, down)
    gate_grad = (hidden_grad * up_pre * gelu_slope(gate_pre)).astype(BF16)
    lift_grad = (hidden_grad * gelu_tanh(gate_pre)).astype(BF16)
    feed_own = scatter(
        jnp.concatenate(
            [
                weight_term(normed_third, gate_grad).astype(BF16),
                weight_term(normed_third, lift_grad).astype(BF16),
            ],
            axis=1,
        )
    )
    third_grad = back_term(gate_grad, gate_proj) + back_term(lift_grad, up_proj)
    carry, gain_third_grad = norm_back(later, scale_third, gain_third, third_grad)
    later_grad = upstream.astype(F32) + carry
    branch_two = later_grad.astype(BF16)
    context_two_grad = back_term(branch_two, out_cross).astype(BF16)
    query_two_grad, kv_two_grad = run_cross_backward(
        query_two, kv_two, context_two_grad, context_two, lse_cross, nseq
    )
    cross_own = scatter(
        jnp.concatenate(
            [
                weight_term(normed_second, query_two_grad).astype(BF16),
                weight_term(memory_rows, kv_two_grad).astype(BF16),
                weight_term(context_two, branch_two).astype(BF16),
            ],
            axis=1,
        )
    )
    memory_grad = back_term(kv_two_grad, kv_cross)
    carry, gain_second_grad = norm_back(
        middle, scale_second, gain_second, back_term(query_two_grad, query_cross)
    )
    middle_grad = later_grad + carry
    branch_one = middle_grad.astype(BF16)
    context_grad = back_term(branch_one, out_self).astype(BF16)
    qkv_grad, diagonal = run_self_backward(
        prefix_len, qkv, context_grad, context, lse_self, bias, nseq
    )
    first_grad = back_term(qkv_grad, qkv_proj)
    carry, gain_first_grad = norm_back(start_rows, scale_first, gain_first, first_grad)
    tokens_grad = middle_grad + carry

    onehot = (
        buckets_back.reshape(-1, 1) == jnp.arange(BUCKETS, dtype=jnp.int32)[None, :]
    ).astype(F32)
    onehot = onehot * (jnp.arange(2 * length) < 2 * length - 1)[:, None]
    bias_grad = jnp.dot(
        diagonal.reshape(NHEAD, 2 * length), onehot, precision=lax.Precision.HIGHEST
    )
    bias_rows = jnp.pad(
        bias_grad.reshape(groups, entries), ((0, 0), (0, shard - entries))
    ).reshape(width)
    vector_block = jnp.pad(
        jnp.stack([gain_first_grad, gain_second_grad, gain_third_grad, bias_rows], axis=0),
        ((0, LANES - 4), (0, 0)),
    ).T
    self_own = scatter(
        jnp.concatenate(
            [
                weight_term(normed_first, qkv_grad).astype(BF16),
                weight_term(context, branch_one).astype(BF16),
                vector_block.astype(BF16),
            ],
            axis=1,
        )
    )

    (down_weight_grad,) = scatter_columns([down_own])
    key_own, value_own = deinterleave(cross_own[:, width : 3 * width], 2)
    gate_g, up_g, cq_g, ck_g, cv_g, co_g = scatter_columns(
        [
            feed_own[:, :ffn],
            feed_own[:, ffn:],
            cross_own[:, :width],
            key_own,
            value_own,
            cross_own[:, 3 * width :],
        ]
    )
    q_own, k_own, v_own = deinterleave(self_own[:, : 3 * width], 3)
    copies = jnp.tile(self_own[:, 4 * width :], (1, lax.axis_size("rep")))
    sq_g, sk_g, sv_g, so_g, vec = scatter_columns(
        [q_own, k_own, v_own, self_own[:, 3 * width : 4 * width], copies]
    )
    return (
        result.reshape(tokens.shape),
        tokens_grad.reshape(tokens.shape),
        memory_grad.reshape(memory.shape),
        vec[:entries, 3],
        vec[:, 0],
        sq_g,
        sk_g,
        sv_g,
        so_g,
        vec[:, 1],
        cq_g,
        ck_g,
        cv_g,
        co_g,
        vec[:, 2],
        gate_g,
        up_g,
        down_weight_grad,
    )


def solution(mesh):
    batch = P(("rep", "fsdp"), None, None)
    matrix = P("fsdp", None)
    vector = P("fsdp")
    split = P("fsdp", "rep")
    in_specs = (
        (batch, batch, P(("rep", "fsdp")), P(), vector, vector)
        + (matrix,) * 4
        + (vector,)
        + (matrix,) * 4
        + (vector,)
        + (matrix,) * 3
        + (batch,)
    )
    out_specs = (
        (batch, batch, batch, vector, vector)
        + (split,) * 4
        + (vector,)
        + (split,) * 4
        + (vector,)
        + (split,) * 3
    )
    return jax.shard_map(body, mesh=mesh, in_specs=in_specs, out_specs=out_specs, check_vma=False)
```

time: 1800 us -> 686 us (0.38)
  waiting for transfers between devices: 690 us -> 212 us
  local copies, waits for them, and re-layouts: 527 us -> 145 us
  matrix products: 355 us -> 145 us
  Pallas kernels: 0 us -> 122 us
  other arithmetic: 127 us -> 35.6 us
  blocking collectives: 70.5 us -> 0 us
    reduce_scatter x14 -> x4, waiting for transfers between devices: 493 us -> 105 us  [the longest x3 77.8 us: scatter(): lax.psum_scatter(block.astype(BF16), 'fsdp', scatter_dimension=0, tiled=T...]
    dot_general x93 -> x25, matrix products: 355 us -> 145 us  [the longest x8 54.2 us: back_term(): lax.dot_general(gradient, weight, LAST_DIMS, preferred_element_type=F32)]
    while x429 -> x0, local copies, waits for them, and re-layouts: 194 us -> none
    reshape x6 -> x9, local copies, waits for them, and re-layouts: 135 us -> 8.24 us  [the longest x5 5.81 us: scatter_columns(): split = [part.reshape(rows, count, -1) for part in parts]]
    pallas_call x0 -> x5, Pallas kernels: none -> 122 us  [the longest x1 35.6 us: run_cross_backward(): pl.pallas_call(cross_backward, grid=(nseq, PAIRS), in_specs=[rows, wide,...]
    unnamed x30 -> x14, waiting for transfers between devices: 115 us -> 54.9 us
    slice x4 -> x21, local copies, waits for them, and re-layouts: 72.3 us -> 25.3 us  [the longest x5 8.6 us: deinterleave(): split[:, :, index].reshape(rows, PAIRS * LANES)]
    convert_element_type x32 -> x10, other arithmetic: 57.3 us -> 10.5 us  [the longest x7 6.07 us: scatter_columns(): outs.append(own[:, start:start + size].astype(F32))]
  transfers between devices with their start and end apart: 44 -> 11, of which waited for: 21 -> 8; matrix products, arithmetic and copies ran while one was open for 37% -> 39% of each run, Pallas kernels for 0% -> 13%
where the time goes in v1:
time: 686 us; the launch traced here: 676 us
  waiting for transfers between devices  212 us (31%)
  local copies, waits for them, and re-layouts  145 us (21%)
  matrix products  145 us (21%)
  Pallas kernels  122 us (18%)
  other arithmetic  35.6 us (5%)
  between operations  15 us (2%)
    unnamed x146, local copies, waits for them, and re-layouts  95.3 us
    reduce_scatter x3, waiting for transfers between devices, scatter(): lax.psum_scatter(block.astype(BF16), 'fsdp', scatter_dimension=0, tiled=T...  77.8 us
    unnamed x14, waiting for transfers between devices  54.9 us
    dot_general x8, matrix products, back_term(): lax.dot_general(gradient, weight, LAST_DIMS, preferred_element_type=F32)  54.2 us
    dot_general x8, matrix products, matmul(): return jnp.dot(left_side, right_side, preferred_element_type=F32)  53.8 us
    all_gather x4, waiting for transfers between devices, gather(): return lax.all_gather(block, 'fsdp', axis=0, tiled=True)  52.6 us
    dot_general x8, matrix products, weight_term(): lax.dot_general(inputs, gradient, FIRST_DIMS, preferred_element_type=F32)  36.4 us
    pallas_call x1, Pallas kernels, run_cross_backward(): pl.pallas_call(cross_backward, grid=(nseq, PAIRS), in_specs=[rows, wide,...  35.6 us
  transfers between devices with their start and end apart: 11, of which 8 were waited for; matrix products, arithmetic and copies ran while one was open for 39% of the time, Pallas kernels for 13%

profile of v1, /device:TPU:0, one launch (start us, length us, event | category | flops | bytes accessed | tf_op | source)
XLA Modules:
  0.0 675.8 jit_solution(3312493580755779802)
XLA Ops:
  92.4 9.0 %fusion.69 = f32[1024,2048]{1,0:T(8,128)} fusion(bf16[1024,768]{1,0:T(8,128)(2,1)} %bitcast.108, bf16[2048,768]{1,0:T(8,128)(2,1)} %all-gather.11.cloned.1.call-done), kind=kOutput, calls=%fused_computation.173 | convolution fusion | flops 3221225472 | bytes 13107200 | tf_op jit(solution)/shard_map/dot_general | solution.py:37
  101.5 10.6 %all-gather.5.cloned.1.call-done = bf16[768,2432]{1,0:T(8,128)(2,1)} async-done(((bf16[96,2432]{1,0:T(8,128)(2,1)}), bf16[768,2432]{1,0:T(8,128)(2,1)}) %all-gather.5.cloned.1.call-update) | async-done | bytes 3735568 | tf_op jit(solution)/shard_map/all_gather | solution.py:422
  114.1 4.9 skewed_bias.1.bias_ref
  123.5 5.6 convolution_convert_fusion.1.qkv_ref
  129.1 22.5 %self_forward.1 = (bf16[1024,768]{1,0:T(8,128)(2,1)}, f32[2,6,2,512]{3,2,1,0:T(2,128)}) custom-call(s32[2]{0:T(128)} %prefix_ref.3, bf16[1024,2304]{1,0:T(8,128)(2,1)} %convolution_convert_fusion.1.qkv_ref, f32[12,128,896]{2,1,0:T(8,128)} %skewed_bias.1.bias_ref), custom_call_target="tpu_custom_call" | custom-call | flops 20000000000 | bytes 12000000 | tf_op jit(solution)/shard_map/self_forward/pallas_call | solution.py:297
  151.6 23.0 %all-gather.7.cloned.1.call-done = bf16[768,3840]{1,0:T(8,128)(2,1)} async-done(((bf16[96,3840]{1,0:T(8,128)(2,1)}), bf16[768,3840]{1,0:T(8,128)(2,1)}) %all-gather.7.cloned.1.call-update) | async-done | bytes 5898256 | tf_op jit(solution)/shard_map/all_gather | solution.py:422
  181.2 6.9 %fusion.7.kv_ref = bf16[2048,1536]{1,0:T(8,128)(2,1)} fusion(bf16[2048,768]{1,0:T(8,128)(2,1)S(1)} %bitcast.101, bf16[768,3840]{1,0:T(8,128)(2,1)S(1)} %copy-done.15), kind=kOutput, calls=%fused_computation.13 | convolution fusion | flops 4834983936 | bytes 11796480 | tf_op jit(solution)/shard_map/dot_general | solution.py:29
  188.2 25.0 %cross_forward.1 = (bf16[1024,768]{1,0:T(8,128)(2,1)}, f32[2,6,2,512]{3,2,1,0:T(2,128)}) custom-call(bf16[1024,768]{1,0:T(8,128)(2,1)} %convolution_convert_fusion.9.query_ref, bf16[2048,1536]{1,0:T(8,128)(2,1)} %fusion.7.kv_ref), custom_call_target="tpu_custom_call" | custom-call | flops 24000000000 | bytes 10000000 | tf_op jit(solution)/shard_map/cross_forward/pallas_call | solution.py:325
  220.6 18.9 %all-gather.9.cloned.1.call-done = bf16[768,4096]{1,0:T(8,128)(2,1)} async-done(((bf16[96,4096]{1,0:T(8,128)(2,1)}), bf16[768,4096]{1,0:T(8,128)(2,1)}) %all-gather.9.cloned.1.call-update) | async-done | bytes 6291472 | tf_op jit(solution)/shard_map/all_gather | solution.py:422
  239.5 9.2 %fusion.25 = f32[1024,2048]{1,0:T(8,128)} fusion(bf16[1024,768]{1,0:T(8,128)(2,1)} %multiply_convert_fusion.2, bf16[768,4096]{1,0:T(8,128)(2,1)} %all-gather.9.cloned.1.call-done), kind=kOutput, calls=%fused_computation.56 | convolution fusion | flops 3221225472 | bytes 13107200 | tf_op jit(solution)/shard_map/dot_general | solution.py:29
  248.7 14.0 %fusion.6 = (bf16[1024,2048]{1,0:T(8,128)(2,1)S(1)}, bf16[1024,2048]{1,0:T(8,128)(2,1)}, bf16[1024,2048]{1,0:T(8,128)(2,1)}) fusion(f32[1024,2048]{1,0:T(8,128)} %fusion.69, f32[1024,2048]{1,0:T(8,128)} %fusion.25, bf16[1024,768]{1,0:T(8,128)(2,1)S(1)} %copy-done.10, bf16[768,4096]{1,0:T(8,128)(2,1)S(1)} %copy-done.28), kind=kOutput, calls=%fused_computation.8 | convolution fusion | flops 3273654272 | bytes 34078720 | tf_op jit(solution)/shard_map/dot_general | solution.py:29
  262.7 7.3 %fusion.23 = f32[1024,768]{1,0:T(8,128)S(1)} fusion(bf16[1024,2048]{1,0:T(8,128)(2,1)} %get-tuple-element.119, bf16[768,4096]{1,0:T(8,128)(2,1)S(1)} %copy-done.28), kind=kOutput, calls=%fused_computation.54 | convolution fusion | flops 3221225472 | bytes 10485760 | tf_op jit(solution)/shard_map/dot_general | solution.py:37
  275.2 4.8 convolution_convert_fusion.8.up_ref
  280.0 35.6 %cross_backward.1 = (bf16[1024,768]{1,0:T(8,128)(2,1)}, bf16[2048,1536]{1,0:T(8,128)(2,1)}) custom-call(bf16[1024,768]{1,0:T(8,128)(2,1)} %convolution_convert_fusion.9.query_ref, bf16[2048,1536]{1,0:T(8,128)(2,1)} %fusion.7.kv_ref, bf16[1024,768]{1,0:T(8,128)(2,1)} %convolution_convert_fusion.8.up_ref, bf16[1024,768]{1,0:T(8,128)(2,1)} %get-tuple-element.27.context_ref, ...), custom_call_target="tpu_custom_call" | custom-call | flops 35999997952 | bytes 20000000 | tf_op jit(solution)/shard_map/cross_backward/pallas_call | solution.py:352
  315.6 6.1 multiply_reduce_fusion.1
  321.7 4.9 convolution_convert_fusion.3
  331.5 4.8 convolution_convert_fusion.7.up_ref
  336.3 34.2 %self_backward.1 = (bf16[1024,2304]{1,0:T(8,128)(2,1)}, f32[6,2,1024]{2,1,0:T(2,128)}) custom-call(s32[2]{0:T(128)} %prefix_ref.3, bf16[1024,2304]{1,0:T(8,128)(2,1)} %convolution_convert_fusion.1.qkv_ref, bf16[1024,768]{1,0:T(8,128)(2,1)} %convolution_convert_fusion.7.up_ref, bf16[1024,768]{1,0:T(8,128)(2,1)} %get-tuple-element.26.context_ref, ...), custom_call_target="tpu_custom_call" | custom-call | flops 24000000000 | bytes 20000000 | tf_op jit(solution)/shard_map/self_backward/pallas_call | solution.py:378
  370.6 9.5 %fusion.18 = (bf16[768]{0:T(1024)(128)(2,1)S(1)}, f32[1024]{0:T(1024)S(1)}, f32[1024,768]{1,0:T(8,128)}) fusion(bf16[2,512,768]{2,1,0:T(8,128)(2,1)} %param.20, f32[1024]{0:T(1024)S(1)} %bitcast.122, f32[768]{0:T(1024)S(1)} %copy-done.18, bf16[1024,2304]{1,0:T(8,128)(2,1)} %get-tuple-element.31, bf16[768,2432]{1,0:T(8,128)(2,1)} %all-gather.5.cloned.1.call-done), kind=kOutput, calls=%fused_computation.38 | convolution fusion | flops 3629381888 | bytes 12988928 | tf_op jit(solution)/shard_map/dot_general | solution.py:37
  385.3 6.5 convolution_convert_fusion.2
  400.7 5.4 fusion.22
  408.6 6.6 copy.175
  415.3 6.3 convolution_convert_fusion.5
  431.3 18.5 %reduce-scatter.14.cloned.1.call-done = bf16[96,3200]{1,0:T(8,128)(2,1)} async-done(((bf16[768,3200]{1,0:T(8,128)(2,1)}), bf16[96,3200]{1,0:T(8,128)(2,1)}) %reduce-scatter.14.cloned.1.call-update) | async-done | bytes 614416 | tf_op jit(solution)/shard_map/reduce_scatter | solution.py:426
  470.9 34.5 %reduce-scatter.24.cloned.1.call-done = bf16[96,3072]{1,0:T(8,128)(2,1)} async-done(((bf16[768,3072]{1,0:T(8,128)(2,1)}), bf16[96,3072]{1,0:T(8,128)(2,1)}) %reduce-scatter.24.cloned.1.call-update) | async-done | bytes 589840
  517.3 59.3 %reduce-scatter.16.cloned.1.call-done = bf16[96,4096]{1,0:T(8,128)(2,1)} async-done(((bf16[768,4096]{1,0:T(8,128)(2,1)}), bf16[96,4096]{1,0:T(8,128)(2,1)}) %reduce-scatter.16.cloned.1.call-update) | async-done | bytes 786448 | tf_op jit(solution)/shard_map/reduce_scatter | solution.py:426
  581.5 5.0 concatenate.31
  589.2 6.1 fusion.14
  595.3 7.2 %add_convert_fusion = bf16[1024,768]{1,0:T(8,128)(2,1)} fusion(f32[1024,768]{1,0:T(8,128)S(1)} %copy-done.3, bf16[1024,2048]{1,0:T(8,128)(2,1)} %get-tuple-element.120, bf16[2048,768]{1,0:T(8,128)(2,1)S(1)} %copy-done.29), kind=kOutput, calls=%fused_computation.45 | convolution fusion | flops 3222798336 | bytes 12058624 | tf_op jit(solution)/shard_map/dot_general | solution.py:29
  602.5 8.6 %fusion.31 = f32[2048,768]{1,0:T(8,128)} fusion(bf16[2048,1536]{1,0:T(8,128)(2,1)S(1)} %bitcast.135, bf16[768,3840]{1,0:T(8,128)(2,1)} %all-gather.7.cloned.1.call-done), kind=kOutput, calls=%fused_computation.62 | convolution fusion | flops 4831838208 | bytes 14942208 | tf_op jit(solution)/shard_map/dot_general | solution.py:37
  612.9 19.5 %reduce-scatter.22.cloned.1.call-done = bf16[896,96]{1,0:T(8,128)(2,1)} async-done(((bf16[3584,96]{1,0:T(8,128)(2,1)}), bf16[896,96]{1,0:T(8,128)(2,1)}) %reduce-scatter.22.cloned.1.call-update) | async-done | bytes 172048
  638.6 26.7 %reduce-scatter.18.cloned.1.call-done = bf16[96,1792]{1,0:T(8,128)(2,1)} async-done(((bf16[96,7168]{1,0:T(8,128)(2,1)}), bf16[96,1792]{1,0:T(8,128)(2,1)}) %reduce-scatter.18.cloned.1.call-update) | async-done | bytes 344080 | tf_op jit(solution)/shard_map/reduce_scatter | solution.py:434
  (254 shorter events, 193.4 us)
Async XLA Ops:
  7.2 174.0 %copy-start = (bf16[2,1024,768]{2,1,0:T(8,128)(2,1)S(1)}, bf16[2,1024,768]{2,1,0:T(8,128)(2,1)}, u32[]{:S(2)}) copy-start(bf16[2,1024,768]{2,1,0:T(8,128)(2,1)} %param.21) | copy-start | bytes 9437188
  7.2 56.2 %copy-start.27 = (bf16[96]{0:T(256)(128)(2,1)S(1)}, bf16[96]{0:T(256)(128)(2,1)}, u32[]{:S(2)}) copy-start(bf16[96]{0:T(256)(128)(2,1)} %param.25) | copy-start | bytes 580
  7.2 56.2 %copy-start.26 = (bf16[96]{0:T(256)(128)(2,1)S(1)}, bf16[96]{0:T(256)(128)(2,1)}, u32[]{:S(2)}) copy-start(bf16[96]{0:T(256)(128)(2,1)} %param.30) | copy-start | bytes 580
  7.2 56.2 %copy-start.25 = (bf16[96]{0:T(256)(128)(2,1)S(1)}, bf16[96]{0:T(256)(128)(2,1)}, u32[]{:S(2)}) copy-start(bf16[96]{0:T(256)(128)(2,1)} %param.35) | copy-start | bytes 580
  7.2 85.2 %all-gather.11.cloned.1.call-start = ((), (), s32[]{:S(2)}) async-start(), calls=%async_computation.10 | async-start | bytes 3538944 | tf_op jit(solution)/shard_map/all_gather | solution.py:422
  8.0 104.1 %all-gather.5.cloned.1.call-start = ((), (), s32[]{:S(2)}) async-start(), calls=%async_computation.7 | async-start | bytes 4202496 | tf_op jit(solution)/shard_map/all_gather | solution.py:422
  11.8 75.4 %copy-start.14 = (bf16[96,2048]{1,0:T(8,128)(2,1)S(1)}, bf16[96,2048]{1,0:T(8,128)(2,1)}, u32[]{:S(2)}) copy-start(bf16[96,2048]{1,0:T(8,128)(2,1)} %param.37) | copy-start | bytes 1179652
  66.2 24.9 %copy-start.23 = (s32[1023]{0:T(1024)S(1)}, s32[1023]{0:T(1024)}, u32[]{:S(2)}) copy-start(s32[1023]{0:T(1024)} %param.23) | copy-start | bytes 12280
  66.2 108.5 %all-gather.7.cloned.1.call-start = ((), (), s32[]{:S(2)}) async-start(), calls=%async_computation.8 | async-start | bytes 6635520 | tf_op jit(solution)/shard_map/all_gather | solution.py:422
  87.2 152.4 %all-gather.9.cloned.1.call-start = ((), (), s32[]{:S(2)}) async-start(), calls=%async_computation.9 | async-start | bytes 7077888 | tf_op jit(solution)/shard_map/all_gather | solution.py:422
  89.2 339.8 %reduce-scatter.20.cloned.1.call-start = ((), (), s32[]{:S(2)}) async-start(), calls=%async_computation.14 | async-start | bytes 3538944 | tf_op jit(solution)/shard_map/reduce_scatter | solution.py:426
  91.1 28.3 %copy-start.19 = (f32[1,4,2,128]{3,1,2,0:T(4,128)}, f32[1,4,2,128]{3,1,2,0:T(4,128)S(1)}, u32[]{:S(2)}) copy-start(f32[1,4,2,128]{3,1,2,0:T(4,128)S(1)} %copy.209) | copy-start | bytes 12292
  239.5 9.2 %copy-start.10 = (bf16[1024,768]{1,0:T(8,128)(2,1)S(1)}, bf16[1024,768]{1,0:T(8,128)(2,1)}, u32[]{:S(2)}) copy-start(bf16[1024,768]{1,0:T(8,128)(2,1)} %multiply_convert_fusion.2) | copy-start | bytes 4718596
  239.5 9.2 %copy-start.28 = (bf16[768,4096]{1,0:T(8,128)(2,1)S(1)}, bf16[768,4096]{1,0:T(8,128)(2,1)}, u32[]{:S(2)}) copy-start(bf16[768,4096]{1,0:T(8,128)(2,1)} %all-gather.9.cloned.1.call-done) | copy-start | bytes 18874372
  262.7 7.3 %copy-start.31 = (bf16[1024,2048]{1,0:T(8,128)(2,1)}, bf16[1024,2048]{1,0:T(8,128)(2,1)S(1)}, u32[]{:S(2)}) copy-start(bf16[1024,2048]{1,0:T(8,128)(2,1)S(1)} %get-tuple-element.118) | copy-start | bytes 12582916
  262.7 7.4 %copy-start.2 = (f32[1024,768]{1,0:T(8,128)S(1)}, f32[1024,768]{1,0:T(8,128)}, u32[]{:S(2)}) copy-start(f32[1024,768]{1,0:T(8,128)} %copy-done.1) | copy-start | bytes 9437188
  326.6 123.2 %reduce-scatter.14.cloned.1.call-start = ((), (), s32[]{:S(2)}) async-start(), calls=%async_computation.11 | async-start | bytes 5529600 | tf_op jit(solution)/shard_map/reduce_scatter | solution.py:426
  336.3 34.2 %copy-start.18 = (f32[768]{0:T(1024)S(1)}, f32[768]{0:T(1024)}, u32[]{:S(2)}) copy-start(f32[768]{0:T(1024)} %copy-done.17) | copy-start | bytes 9220
  336.3 34.2 %copy-start.20 = (f32[1,4,2,128]{3,1,2,0:T(4,128)S(1)}, f32[1,4,2,128]{3,1,2,0:T(4,128)}, u32[]{:S(2)}) copy-start(f32[1,4,2,128]{3,1,2,0:T(4,128)} %copy-done.19) | copy-start | bytes 12292
  370.6 9.6 %copy-start.16 = (f32[6,2,1024]{2,1,0:T(2,128)S(1)}, f32[6,2,1024]{2,1,0:T(2,128)}, u32[]{:S(2)}) copy-start(f32[6,2,1024]{2,1,0:T(2,128)} %get-tuple-element.33) | copy-start | bytes 147460
  370.6 9.6 %copy-start.21 = (s32[1024]{0:T(1024)S(1)}, s32[1024]{0:T(1024)}, u32[]{:S(2)}) copy-start(s32[1024]{0:T(1024)} %pad.29) | copy-start | bytes 12292
  370.6 9.6 %copy-start.24 = (f32[1024]{0:T(1024)S(1)}, f32[1024]{0:T(1024)}, u32[]{:S(2)}) copy-start(f32[1024]{0:T(1024)} %fusion.59) | copy-start | bytes 12292
  394.2 111.2 %reduce-scatter.24.cloned.1.call-start = ((), (), s32[]{:S(2)}) async-start(), calls=%async_computation.16 | async-start | bytes 5308416
  415.3 161.3 %reduce-scatter.16.cloned.1.call-start = ((), (), s32[]{:S(2)}) async-start(), calls=%async_computation.12 | async-start | bytes 7077888 | tf_op jit(solution)/shard_map/reduce_scatter | solution.py:426
  415.3 6.4 copy-start.11
  415.3 6.4 copy-start.32
  428.9 182.2 %reduce-scatter.26.cloned.1.call-start = ((), (), s32[]{:S(2)}) async-start(), calls=%async_computation.17 | async-start | bytes 491520
  431.0 201.5 %reduce-scatter.22.cloned.1.call-start = ((), (), s32[]{:S(2)}) async-start(), calls=%async_computation.15 | async-start | bytes 1146880
  449.8 14.5 %slice-start = ((bf16[96,3200]{1,0:T(8,128)(2,1)}), bf16[96,128]{1,0:T(8,128)(2,1)S(1)}, s32[]{:S(2)}) async-start(bf16[96,3200]{1,0:T(8,128)(2,1)} %reduce-scatter.14.cloned.1.call-done), calls=%async_computation.18 | async-start | bytes 49152 | tf_op jit(solution)/shard_map/slice | solution.py:607
  470.8 194.5 %reduce-scatter.18.cloned.1.call-start = ((), (), s32[]{:S(2)}) async-start(), calls=%async_computation.13 | async-start | bytes 1720320 | tf_op jit(solution)/shard_map/reduce_scatter | solution.py:434
  589.2 13.3 %slice-start.3 = ((s8[6291456]{0:T(1024)(128)(4,1)}), s8[4194304]{0:T(1024)(128)(4,1)S(1)}, s32[]{:S(2)}) async-start(s8[6291456]{0:T(1024)(128)(4,1)} %bitcast.134), calls=%async_computation.21 | async-start | bytes 8388608
  595.3 7.2 %slice-start.4 = ((s8[6291456]{0:T(1024)(128)(4,1)}), s8[2097152]{0:T(1024)(128)(4,1)S(1)}, s32[]{:S(2)}) async-start(s8[6291456]{0:T(1024)(128)(4,1)} %bitcast.134), calls=%async_computation.22 | async-start | bytes 4194304
  (18 other events, 72.6 us)
Sparse Core Ops, SparseCore 0:
  9.7 40.8 all-gather.10
  66.3 45.7 all-gather.4
  114.3 60.2 all-gather.6
  176.1 63.3 all-gather.8
  326.7 39.0 reduce-scatter.19
  394.3 55.4 reduce-scatter.13
  452.1 53.3 reduce-scatter.23
  508.3 68.1 reduce-scatter.15
  579.4 23.1 reduce-scatter.25
  605.4 27.0 reduce-scatter.21
  635.4 29.9 reduce-scatter.17

commit v2 on v1

--- a/solution.py
+++ b/solution.py
@@ -118,13 +118,13 @@
     )(jnp.pad(table, ((0, 4), (0, 0))), buckets_back)
 
 
-def self_forward(prefix_ref, qkv_ref, bias_ref, out_ref, lse_ref):
-    length = qkv_ref.shape[0]
+def self_forward(prefix_ref, query_ref, key_ref, value_ref, bias_ref, out_ref, lse_ref):
+    length = query_ref.shape[0]
     block = 256
     prefix = prefix_ref[pl.program_id(0)]
-    queries = qkv_ref[:, :LANES]
-    keys = qkv_ref[:, LANES : 2 * LANES]
-    values = flipped(qkv_ref[:, 2 * LANES :])
+    queries = query_ref[...]
+    keys = key_ref[...]
+    values = flipped(value_ref[...])
     for start in range(0, length, block):
         stop = start + block
         count = max(PREFIX_MAX, stop)
@@ -156,10 +156,9 @@
         out_ref[start:stop, :] = jnp.concatenate(outs, axis=0).T.astype(BF16)
 
 
-def cross_forward(query_ref, kv_ref, out_ref, lse_ref):
-    length = query_ref.shape[0]
-    keys = kv_ref[:, :LANES]
-    values = flipped(kv_ref[:, LANES:])
+def cross_forward(query_ref, key_ref, value_ref, out_ref, lse_ref):
+    keys = key_ref[...]
+    values = flipped(value_ref[...])
     queries = query_ref[...]
     ahead = [back_term(keys, one_head(queries, head)) for head in range(2)]
     outs = []
@@ -174,11 +173,13 @@
     out_ref[...] = jnp.concatenate(outs, axis=0).T.astype(BF16)
 
 
-def cross_backward(query_ref, kv_ref, up_ref, context_ref, lse_ref, dq_ref, dkv_ref):
+def cross_backward(
+    query_ref, key_ref, value_ref, up_ref, context_ref, lse_ref, dq_ref, dk_ref, dv_ref
+):
     length = query_ref.shape[0]
     block = 256
-    keys = kv_ref[:, :LANES]
-    values = kv_ref[:, LANES:]
+    keys = key_ref[...]
+    values = value_ref[...]
     queries = query_ref[...]
     upstream = up_ref[...]
     keys_flipped = flipped(keys)
@@ -202,14 +203,26 @@
             key_grad = key_part if key_grad is None else key_grad + key_part
             grads.append(matmul(keys_flipped[sub], score_grad))
         dq_ref[rows, :] = jnp.concatenate(grads, axis=0).T.astype(BF16)
-    dkv_ref[:, :LANES] = key_grad.astype(BF16)
-    dkv_ref[:, LANES:] = value_grad.astype(BF16)
+    dk_ref[...] = key_grad.astype(BF16)
+    dv_ref[...] = value_grad.astype(BF16)
 
 
 def self_backward(
-    prefix_ref, qkv_ref, up_ref, context_ref, lse_ref, bias_ref, grad_ref, diag_ref, acc_ref
+    prefix_ref,
+    query_ref,
+    key_ref,
+    value_ref,
+    up_ref,
+    context_ref,
+    lse_ref,
+    bias_ref,
+    dq_ref,
+    dk_ref,
+    dv_ref,
+    diag_ref,
+    acc_ref,
 ):
-    length = qkv_ref.shape[0]
+    length = query_ref.shape[0]
     block = 256
     step = pl.program_id(1)
     prefix = prefix_ref[step]
@@ -218,9 +231,9 @@
     def _():
         acc_ref[...] = jnp.zeros_like(acc_ref)
 
-    queries = qkv_ref[:, :LANES]
-    keys = qkv_ref[:, LANES : 2 * LANES]
-    values = qkv_ref[:, 2 * LANES :]
+    queries = query_ref[...]
+    keys = key_ref[...]
+    values = value_ref[...]
     upstream = up_ref[...]
     keys_flipped = flipped(keys)
     inner = (upstream.astype(F32) * context_ref[...].astype(F32)).T
@@ -267,11 +280,11 @@
                     value_grad[index] = value_grad[index] + value_part[part]
                     key_grad[index] = key_grad[index] + key_part[part]
             grads.append(matmul(keys_flipped[sub, :count], score_grad))
-        grad_ref[rows, :LANES] = jnp.concatenate(grads, axis=0).T.astype(BF16)
+        dq_ref[rows, :] = jnp.concatenate(grads, axis=0).T.astype(BF16)
     for index in range(count_all):
         part = slice(index * block, (index + 1) * block)
-        grad_ref[part, LANES : 2 * LANES] = key_grad[index].astype(BF16)
-        grad_ref[part, 2 * LANES :] = value_grad[index].astype(BF16)
+        dk_ref[part, :] = key_grad[index].astype(BF16)
+        dv_ref[part, :] = value_grad[index].astype(BF16)
 
     @pl.when(step == pl.num_programs(1) - 1)
     def _():
@@ -300,7 +313,9 @@
             num_scalar_prefetch=1,
             grid=(nseq, PAIRS),
             in_specs=[
-                spec((length, 3 * LANES), lambda s, p, _: (s, p)),
+                spec((length, LANES), lambda s, p, _: (s, p)),
+                spec((length, LANES), lambda s, p, _: (s, PAIRS + p)),
+                spec((length, LANES), lambda s, p, _: (s, 2 * PAIRS + p)),
                 spec((2, LANES, 2 * length - LANES), lambda s, p, _: (p, 0, 0)),
             ],
             out_specs=[
@@ -316,7 +331,7 @@
             flops=20_000_000_000, bytes_accessed=12_000_000, transcendentals=0
         ),
         name="self_forward",
-    )(prefix, qkv, bias)
+    )(prefix, qkv, qkv, qkv, bias)
 
 
 def run_cross_forward(query, kv, nseq):
@@ -327,7 +342,8 @@
         grid=(nseq, PAIRS),
         in_specs=[
             spec((length, LANES), lambda s, p: (s, p)),
-            spec((count, 2 * LANES), lambda s, p: (s, p)),
+            spec((count, LANES), lambda s, p: (s, p)),
+            spec((count, LANES), lambda s, p: (s, PAIRS + p)),
         ],
         out_specs=[
             spec((length, LANES), lambda s, p: (s, p)),
@@ -341,85 +357,737 @@
             flops=24_000_000_000, bytes_accessed=10_000_000, transcendentals=0
         ),
         name="cross_forward",
-    )(query, kv)
+    )(query, kv, kv)
 
 
 def run_cross_backward(query, kv, upstream, context, lse, nseq):
     length = query.shape[0] // nseq
     count = kv.shape[0] // nseq
     rows = spec((length, LANES), lambda s, p: (s, p))
-    wide = spec((count, 2 * LANES), lambda s, p: (s, p))
+    wide = spec((count, LANES), lambda s, p: (s, p))
     return pl.pallas_call(
         cross_backward,
         grid=(nseq, PAIRS),
         in_specs=[
             rows,
             wide,
+            spec((count, LANES), lambda s, p: (s, PAIRS + p)),
             rows,
             rows,
             spec((None, None, 2, length), lambda s, p: (s, p, 0, 0)),
         ],
-        out_specs=[rows, wide],
+        out_specs=[rows, wide, wide],
         out_shape=[
             jax.ShapeDtypeStruct(query.shape, BF16),
-            jax.ShapeDtypeStruct(kv.shape, BF16),
+            jax.ShapeDtypeStruct((kv.shape[0], PAIRS * LANES), BF16),
+            jax.ShapeDtypeStruct((kv.shape[0], PAIRS * LANES), BF16),
         ],
         cost_estimate=pl.CostEstimate(
             flops=36_000_000_000, bytes_accessed=20_000_000, transcendentals=0
         ),
         name="cross_backward",
-    )(query, kv, upstream, context, lse)
+    )(query, kv, kv, upstream, context, lse)
 
 
 def run_self_backward(prefix, qkv, upstream, context, lse, bias, nseq):
     length = qkv.shape[0] // nseq
     rows = spec((length, LANES), lambda p, s, _: (s, p))
-    wide = spec((length, 3 * LANES), lambda p, s, _: (s, p))
     return pl.pallas_call(
         self_backward,
         grid_spec=pltpu.PrefetchScalarGridSpec(
             num_scalar_prefetch=1,
             grid=(PAIRS, nseq),
             in_specs=[
-                wide,
+                rows,
+                spec((length, LANES), lambda p, s, _: (s, PAIRS + p)),
+                spec((length, LANES), lambda p, s, _: (s, 2 * PAIRS + p)),
                 rows,
                 rows,
                 spec((None, None, 2, length), lambda p, s, _: (s, p, 0, 0)),
                 spec((2, LANES, 2 * length - LANES), lambda p, s, _: (p, 0, 0)),
             ],
             out_specs=[
-                wide,
+                rows,
+                rows,
+                rows,
                 spec((None, 2, 2 * length), lambda p, s, _: (p, 0, 0)),
             ],
             scratch_shapes=[pltpu.VMEM((2, LANES, 2 * length - LANES), F32)],
         ),
-        out_shape=[
-            jax.ShapeDtypeStruct(qkv.shape, BF16),
-            jax.ShapeDtypeStruct((PAIRS, 2, 2 * length), F32),
-        ],
+        out_shape=[jax.ShapeDtypeStruct(upstream.shape, BF16)] * 3
+        + [jax.ShapeDtypeStruct((PAIRS, 2, 2 * length), F32)],
         cost_estimate=pl.CostEstimate(
             flops=24_000_000_000, bytes_accessed=20_000_000, transcendentals=0
         ),
         name="self_backward",
-    )(prefix, qkv, upstream, context, lse, bias)
-
-
-def interleave(*parts):
+    )(prefix, qkv, qkv, qkv, upstream, context, lse, bias)
+
+
+MESH = pl.DeviceIdType.MESH
+
+
+class Place:
+    def __init__(self, line):
+        self.line = line
+        rep = lax.axis_index("rep")
+        fsdp = lax.axis_index("fsdp")
+        self.rep = rep
+        self.fsdp = fsdp
+        self.y = rep // 2
+        self.x = rep % 2
+        self.z = fsdp // 2
+        self.core = fsdp % 2
+        self.x_rep = self.y * 2 + 1 - self.x
+        self.y_rep = (1 - self.y) * 2 + self.x
+
+    def at_x(self):
+        return {"rep": self.x_rep, "fsdp": self.fsdp}
+
+    def at_y(self):
+        return {"rep": self.y_rep, "fsdp": self.fsdp}
+
+    def at_partner(self):
+        return {"rep": self.rep, "fsdp": self.z * 2 + 1 - self.core}
+
+    def at_line(self, side):
+        return {"rep": self.rep, "fsdp": self.fsdp + (2 if side == 0 else -2)}
+
+    def has_next(self, side):
+        return self.z < self.line - 1 if side == 0 else self.z > 0
+
+    def has_last(self, side):
+        return self.has_next(1 - side)
+
+    def arrives(self, side, hop):
+        if side == 0:
+            return self.z - 1 - hop >= 0
+        return self.z + 1 + hop <= self.line - 1
+
+    def source(self, side, hop):
+        return self.z - 1 - hop if side == 0 else self.z + 1 + hop
+
+    def at_far(self):
+        half = self.line // 2
+        return {"rep": self.rep, "fsdp": (self.z + half) % self.line * 2 + self.core}
+
+    def greet(self, wide=False):
+        barrier = pltpu.get_barrier_semaphore()
+        targets = [self.at_x(), self.at_y(), self.at_partner()]
+        if wide:
+            targets.append({"rep": 3 - self.rep, "fsdp": self.fsdp})
+            targets.append(self.at_far())
+        for target in targets:
+            pl.semaphore_signal(barrier, inc=1, device_id=target, device_id_type=MESH)
+        for side in range(2):
+
+            @pl.when(self.has_next(side))
+            def _():
+                pl.semaphore_signal(
+                    barrier, inc=1, device_id=self.at_line(side), device_id_type=MESH
+                )
+
+        count = len(targets)
+        for side in range(2):
+            count = count + jnp.where(self.has_next(side), 1, 0)
+        pl.semaphore_wait(barrier, count)
+
+
+def remote(source, target, send, recv, device):
+    return pltpu.make_async_remote_copy(
+        src_ref=source,
+        dst_ref=target,
+        send_sem=send,
+        recv_sem=recv,
+        device_id=device,
+        device_id_type=MESH,
+    )
+
+
+class GatherShape:
+    def __init__(self, rows, columns, by_rows):
+        self.rows = rows
+        self.columns = columns
+        self.by_rows = by_rows
+
+    def full(self, ref, owner):
+        return ref.at[pl.ds(pl.multiple_of(owner * self.rows, 32), self.rows)]
+
+    def piece(self, ref, owner, part, half=None):
+        base = owner * self.rows
+        if self.by_rows:
+            rows = self.rows // 4
+            base = base + part * rows
+        else:
+            rows = self.rows
+        if half is not None:
+            rows = rows // 2
+            base = base + half * rows
+        row_slice = pl.ds(pl.multiple_of(base, 16), rows)
+        if self.by_rows:
+            return ref.at[row_slice]
+        width = self.columns // 4
+        return ref.at[row_slice, pl.ds(pl.multiple_of(part * width, LANES), width)]
+
+
+def gather_sems(line):
+    hops = line - 1
+    return [pltpu.SemaphoreType.DMA((5, 2, 2, hops)), pltpu.SemaphoreType.DMA((4,))] + [
+        pltpu.SemaphoreType.DMA((2, 2, hops))
+    ]
+
+
+def gather_steps(place, shape, src, own, dst, sems):
+    hop_sem, own_sem, pair_sem = sems
+    hops = place.line - 1
+    me = place.fsdp
+
+    def load():
+        return pltpu.make_async_copy(src, own, own_sem.at[0])
+
+    def keep():
+        return pltpu.make_async_copy(own, shape.full(dst, me), own_sem.at[1])
+
+    def own_pair():
+        return remote(
+            own, shape.full(dst, me), own_sem.at[2], own_sem.at[3], place.at_partner()
+        )
+
+    def owner(side, hop):
+        return place.source(side, hop) * 2 + place.core
+
+    def line_first(side):
+        return remote(
+            shape.piece(own, 0, place.rep),
+            shape.piece(dst, me, place.rep),
+            hop_sem.at[0, 0, side, 0],
+            hop_sem.at[0, 1, side, 0],
+            place.at_line(side),
+        )
+
+    def moved(kind, side, hop, block, device):
+        return remote(
+            block, block, hop_sem.at[kind, 0, side, hop], hop_sem.at[kind, 1, side, hop], device
+        )
+
+    def line_next(side, hop):
+        block = shape.piece(dst, owner(side, hop - 1), place.rep)
+        return moved(0, side, hop, block, place.at_line(side))
+
+    def line_arrival(side, hop):
+        block = shape.piece(dst, owner(side, hop), place.rep)
+        return moved(0, side, hop, block, place.at_line(side))
+
+    def plane(axis, side, hop):
+        block = shape.piece(dst, owner(side, hop), place.rep)
+        return moved(1 + axis, side, hop, block, place.at_x() if axis == 0 else place.at_y())
+
+    def cross(axis, side, hop):
+        part = place.x_rep if axis == 1 else place.y_rep
+        block = shape.piece(dst, owner(side, hop), part, 1 - axis)
+        return moved(3 + axis, side, hop, block, place.at_x() if axis == 0 else place.at_y())
+
+    def pair(side, hop):
+        block = shape.full(dst, owner(side, hop))
+        return remote(
+            block, block, pair_sem.at[0, side, hop], pair_sem.at[1, side, hop], place.at_partner()
+        )
+
+    def each(fn):
+        def run():
+            for hop in range(hops):
+                for side in range(2):
+                    pl.when(place.arrives(side, hop))(functools.partial(fn, side, hop))
+
+        return run
+
+    def start():
+        load().start()
+        load().wait()
+        for side in range(2):
+            pl.when(place.has_next(side))(lambda side=side: line_first(side).start())
+        own_pair().start()
+        keep().start()
+
+    def arrive(side, hop):
+        line_arrival(side, hop).wait_recv()
+        if hop + 1 < hops:
+            pl.when(place.has_next(side))(lambda: line_next(side, hop + 1).start())
+        plane(0, side, hop).start()
+        plane(1, side, hop).start()
+
+    def turn(side, hop):
+        plane(0, side, hop).wait_recv()
+        cross(1, side, hop).start()
+        plane(1, side, hop).wait_recv()
+        cross(0, side, hop).start()
+
+    def hand(side, hop):
+        cross(0, side, hop).wait_recv()
+        cross(1, side, hop).wait_recv()
+        pair(side, hop).start()
+
+    def finish():
+        def last(side, hop):
+            pair(side, hop).wait()
+            for axis in range(2):
+                plane(axis, side, hop).wait_send()
+                cross(axis, side, hop).wait_send()
+            if hop + 1 < hops:
+                pl.when(place.has_next(side))(lambda: line_next(side, hop + 1).wait_send())
+
+        each(last)()
+        for side in range(2):
+            pl.when(place.has_next(side))(lambda side=side: line_first(side).wait_send())
+        own_pair().wait()
+        keep().wait()
+
+    return start, each(arrive), each(turn), each(hand), finish
+
+
+def gather_kernel(shapes, line, *refs):
+    count = len(shapes)
+    sources = refs[:count]
+    targets = refs[count : 2 * count]
+    scratch = refs[2 * count :]
+    place = Place(line)
+    place.greet()
+    plans = []
+    for index, shape in enumerate(shapes):
+        own, *sems = scratch[4 * index : 4 * index + 4]
+        plans.append(gather_steps(place, shape, sources[index], own, targets[index], sems))
+    for stage in range(5):
+        for plan in plans:
+            plan[stage]()
+
+
+def fast_gather(blocks, line, by_rows, collective_id):
+    shapes = [
+        GatherShape(block.shape[0], block.shape[1], flag) for block, flag in zip(blocks, by_rows)
+    ]
+    scratch = []
+    for shape in shapes:
+        scratch.append(pltpu.VMEM((shape.rows, shape.columns), BF16))
+        scratch.extend(gather_sems(line))
+    anywhere = pl.BlockSpec(memory_space=pl.ANY)
+    return pl.pallas_call(
+        functools.partial(gather_kernel, shapes, line),
+        in_specs=[anywhere] * len(blocks),
+        out_specs=[anywhere] * len(blocks),
+        out_shape=[
+            jax.ShapeDtypeStruct((2 * line * s.rows, s.columns), BF16) for s in shapes
+        ],
+        scratch_shapes=scratch,
+        compiler_params=pltpu.CompilerParams(collective_id=collective_id, has_side_effects=True),
+        name="fast_gather",
+    )(*blocks)
+
+
+class ReduceShape:
+    def __init__(self, kind, rows, columns, sources):
+        self.kind = kind
+        self.rows = rows
+        self.sources = sources
+        if kind == "rows":
+            self.block = (rows // 8, columns)
+        elif kind == "pair":
+            self.block = (rows // 2, columns // 2)
+        else:
+            self.block = (rows // 2, columns)
+        self.exchange = kind != "pair"
+        self.part_rows = rows // 4 if kind == "rows" else rows
+        self.part_columns = columns // 4
+
+    def pieces(self, refs, owner, half, quarter):
+        rows, columns = self.block
+        if self.kind == "rows":
+            base = owner * self.rows + quarter * (self.rows // 4) + half * rows
+            return [(refs[0].at[pl.ds(pl.multiple_of(base, 16), rows)], 0, columns)]
+        at = pl.ds(pl.multiple_of(owner * self.rows + half * rows, 16), rows)
+        if self.kind == "four":
+            return [(refs[quarter].at[at], 0, columns)]
+        width = columns // 2
+        cut = slice(quarter * width, (quarter + 1) * width)
+        return [(refs[index].at[at, cut], index * width, width) for index in range(2)]
+
+    def out_shape(self):
+        if self.exchange:
+            return jax.ShapeDtypeStruct((4, self.part_rows, self.part_columns), F32)
+        return jax.ShapeDtypeStruct((self.rows, self.block[1]), F32)
+
+    def scratch(self, line):
+        rows, columns = self.block
+        dma = pltpu.SemaphoreType.DMA
+        buffers = [
+            pltpu.VMEM((line, 8, rows, columns), BF16),
+            pltpu.VMEM((line, 8, rows, columns), BF16),
+            pltpu.VMEM((line, 2, 2, rows, columns), BF16),
+            pltpu.VMEM((line, 2, rows, columns), BF16),
+            pltpu.VMEM((line, 2, rows, columns), BF16),
+            pltpu.VMEM((2, line, 2, rows, columns), BF16),
+            pltpu.VMEM((4, self.part_rows, self.part_columns), F32),
+            pltpu.VMEM((4, self.part_rows, self.part_columns), F32),
+            dma((line,)),
+            dma((2, line)),
+            dma((2, line, 2)),
+            dma((2, line, 2)),
+            dma((2, 2, line)),
+            dma((2, 3)),
+        ]
+        return buffers
+
+
+REDUCE_SCRATCH = 14
+
+
+def added(left, right):
+    return (left.astype(F32) + right.astype(F32)).astype(BF16)
+
+
+def reduce_steps(place, shape, refs, out, scratch):
+    own, other, first_in, second_in, total, line_in, parts, gathered = scratch[:8]
+    load_sem, pair_sem, first_sem, second_sem, line_sem, swap_sem = scratch[8:]
+    line = place.line
+    near = (place.x, place.y)
+    far = (place.y, place.x)
+    near_device = (place.at_x(), place.at_y())
+    far_device = (place.at_y(), place.at_x())
+
+    def quarter_of(half, index):
+        high, low = index // 2, index % 2
+        return low * 2 + high if half == 0 else high * 2 + low
+
+    def start(z):
+        for half in range(2):
+            for index in range(4):
+                quarter = quarter_of(half, index)
+                slot = half * 4 + index
+                mine = shape.pieces(refs, 2 * z + place.core, half, quarter)
+                theirs = shape.pieces(refs, 2 * z + 1 - place.core, half, quarter)
+                for (view, column, width), (view_two, _, _) in zip(mine, theirs):
+                    cut = pl.ds(column, width)
+                    remote(
+                        view_two,
+                        other.at[z, slot, :, cut],
+                        pair_sem.at[0, z],
+                        pair_sem.at[1, z],
+                        place.at_partner(),
+                    ).start()
+                    pltpu.make_async_copy(
+                        view, own.at[z, slot, :, cut], load_sem.at[z]
+                    ).start()
+
+    def pair_all(z):
+        return remote(
+            own.at[z], other.at[z], pair_sem.at[0, z], pair_sem.at[1, z], place.at_partner()
+        )
+
+    def first(z, half):
+        return remote(
+            own.at[z, pl.ds(half * 4 + (1 - near[half]) * 2, 2)],
+            first_in.at[z, half],
+            first_sem.at[0, z, half],
+            first_sem.at[1, z, half],
+            near_device[half],
+        )
+
+    def second(z, half):
+        return remote(
+            own.at[z, half * 4 + near[half] * 2 + 1 - far[half]],
+            second_in.at[z, half],
+            second_sem.at[0, z, half],
+            second_sem.at[1, z, half],
+            far_device[half],
+        )
+
+    def along(z, side):
+        return remote(
+            total.at[z],
+            line_in.at[side, z],
+            line_sem.at[0, side, z],
+            line_sem.at[1, side, z],
+            place.at_line(side),
+        )
+
+    def pair_add(z):
+        pltpu.make_async_copy(own.at[z], own.at[z], load_sem.at[z]).wait()
+        pair_all(z).wait_recv()
+
+        @pl.loop(0, 8)
+        def _(slot):
+            own[z, slot] = added(own[z, slot], other[z, slot])
+
+        for half in range(2):
+            first(z, half).start()
+
+    def first_add(z):
+        for half in range(2):
+            first(z, half).wait_recv()
+            base = half * 4 + near[half] * 2
+
+            @pl.loop(0, 2)
+            def _(index):
+                own[z, base + index] = added(own[z, base + index], first_in[z, half, index])
+
+            second(z, half).start()
+
+    def second_add(z):
+        for half in range(2):
+            second(z, half).wait_recv()
+            mine = half * 4 + near[half] * 2 + far[half]
+            total[z, half] = added(own[z, mine], second_in[z, half])
+
+    def line_send(z, side):
+        ahead = place.z < z if side == 0 else place.z > z
+
+        @pl.when(ahead)
+        def _():
+            @pl.when(place.has_last(side))
+            def _():
+                along(z, side).wait_recv()
+
+                @pl.loop(0, 2)
+                def _(half):
+                    total[z, half] = added(total[z, half], line_in[side, z, half])
+
+            along(z, side).start()
+
+    def line_end(z):
+        @pl.when(place.z == z)
+        def _():
+            for side in range(2):
+                pl.when(place.has_last(side))(lambda: along(z, side).wait_recv())
+
+    def swap(rep_slot, device, index):
+        return remote(
+            parts.at[rep_slot],
+            gathered.at[place.rep],
+            swap_sem.at[0, index],
+            swap_sem.at[1, index],
+            device,
+        )
+
+    def swaps():
+        corner = 3 - place.rep
+        return [
+            swap(place.x_rep, place.at_x(), 0),
+            swap(place.y_rep, place.at_y(), 1),
+            swap(corner, {"rep": corner, "fsdp": place.fsdp}, 2),
+        ]
+
+    def finish():
+        rows, columns = shape.block
+        me = place.z
+        for half in range(2):
+            result = total[me, half].astype(F32)
+            for side in range(2):
+                extra = line_in[side, me, half].astype(F32)
+                result = result + jnp.where(place.has_last(side), extra, 0.0)
+            at = slice(half * rows, (half + 1) * rows)
+            if shape.exchange:
+                width = shape.part_columns
+                for index in range(4):
+                    parts[index, at, :] = result[:, index * width : (index + 1) * width]
+            else:
+                out[at, :] = result
+        if shape.exchange:
+            for copy in swaps():
+                copy.start()
+            gathered[place.rep] = parts[place.rep]
+
+    def drain():
+        if shape.exchange:
+            for copy in swaps():
+                copy.wait()
+            out[...] = gathered[...]
+        for z in range(line):
+            pair_all(z).wait_send()
+            for half in range(2):
+                first(z, half).wait_send()
+                second(z, half).wait_send()
+            for side in range(2):
+                ahead = place.z < z if side == 0 else place.z > z
+                pl.when(ahead)(lambda: along(z, side).wait_send())
+
+    order = [line - 1, 0] + [z for z in range(line - 2, 0, -1)]
+
+    def begin():
+        for z in order:
+            start(z)
+
+    def pairs():
+        for z in order:
+            pair_add(z)
+
+    def firsts():
+        for z in order:
+            first_add(z)
+
+    def seconds():
+        for index, z in enumerate(order):
+            second_add(z)
+            if index > 0:
+                line_send(order[index - 1], 0)
+                line_send(order[index - 1], 1)
+        line_send(order[-1], 0)
+        line_send(order[-1], 1)
+
+    def close():
+        for z in range(line):
+            line_end(z)
+        finish()
+
+    return begin, pairs, firsts, seconds, close, drain
+
+
+class VectorSum:
+    def __init__(self, place, source, out, scratch):
+        self.place = place
+        self.source = source
+        self.out = out
+        self.current, self.incoming, self.sems = scratch
+        side = place.z % 2
+        near = place.fsdp + 2 - 4 * side
+        self.devices = [
+            place.at_partner(),
+            place.at_x(),
+            place.at_y(),
+            {"rep": place.rep, "fsdp": near},
+            place.at_far(),
+        ]
+
+    @staticmethod
+    def scratch(shape):
+        return [
+            pltpu.VMEM((6,) + shape, F32),
+            pltpu.VMEM((5,) + shape, F32),
+            pltpu.SemaphoreType.DMA((2, 5)),
+        ]
+
+    def copy(self, index):
+        return remote(
+            self.current.at[index],
+            self.incoming.at[index],
+            self.sems.at[0, index],
+            self.sems.at[1, index],
+            self.devices[index],
+        )
+
+    def round(self, index):
+        if index == 0:
+            self.current[0] = self.source[...]
+        else:
+            self.copy(index - 1).wait_recv()
+            self.current[index] = self.current[index - 1] + self.incoming[index - 1]
+        if index < 5:
+            self.copy(index).start()
+
+    def finish(self):
+        self.out[...] = self.current[5]
+        for index in range(5):
+            self.copy(index).wait_send()
+
+
+def reduce_kernel(shapes, line, vector_count, *refs):
+    sources = []
+    at = 0
+    for shape in shapes:
+        sources.append(refs[at : at + shape.sources])
+        at += shape.sources
+    vector_refs = refs[at : at + vector_count]
+    at += vector_count
+    outs = refs[at : at + len(shapes)]
+    at += len(shapes)
+    vector_outs = refs[at : at + vector_count]
+    at += vector_count
+    place = Place(line)
+    place.greet(wide=True)
+    plans = []
+    for index, shape in enumerate(shapes):
+        part = refs[at : at + REDUCE_SCRATCH]
+        at += REDUCE_SCRATCH
+        plans.append(reduce_steps(place, shape, sources[index], outs[index], part))
+    vectors = []
+    if vector_count:
+        vectors = [VectorSum(place, vector_refs[0], vector_outs[0], refs[at : at + 3])]
+
+    def rounds(*indices):
+        for vector in vectors:
+            for index in indices:
+                vector.round(index)
+
+    rounds(0)
+    for plan in plans:
+        plan[0]()
+    plans[0][1]()
+    rounds(1)
+    plans[0][2]()
+    rounds(2)
+    for index, plan in enumerate(plans):
+        ahead = plans[index + 1] if index + 1 < len(plans) else None
+        if ahead is not None:
+            ahead[1]()
+        plan[3]()
+        if ahead is not None:
+            ahead[2]()
+    rounds(3)
+    for plan in plans:
+        plan[4]()
+    rounds(4, 5)
+    for plan in plans:
+        plan[5]()
+    for vector in vectors:
+        vector.finish()
+
+
+def fast_reduce(groups, kinds, line, collective_id, vector=None):
+    shapes = []
     blocks = []
-    for pair in range(PAIRS):
-        for part in parts:
-            blocks.append(part[:, pair * LANES : (pair + 1) * LANES])
-    return jnp.concatenate(blocks, axis=1)
-
-
-def deinterleave(block, count):
-    rows = block.shape[0]
-    split = block.reshape(rows, PAIRS, count, LANES)
-    return [split[:, :, index].reshape(rows, PAIRS * LANES) for index in range(count)]
+    scratch = []
+    for group, kind in zip(groups, kinds):
+        rows, columns = group[0].shape
+        shape = ReduceShape(kind, rows // (2 * line), columns, len(group))
+        shapes.append(shape)
+        blocks.extend(group)
+        scratch.extend(shape.scratch(line))
+    anywhere = pl.BlockSpec(memory_space=pl.ANY)
+    local = pl.BlockSpec(memory_space=pltpu.VMEM)
+    in_specs = [anywhere] * len(blocks)
+    out_shape = [shape.out_shape() for shape in shapes]
+    if vector is not None:
+        blocks.append(vector)
+        in_specs.append(local)
+        out_shape.append(jax.ShapeDtypeStruct(vector.shape, F32))
+        scratch.extend(VectorSum.scratch(vector.shape))
+    return pl.pallas_call(
+        functools.partial(reduce_kernel, shapes, line, 0 if vector is None else 1),
+        in_specs=in_specs,
+        out_specs=[local] * len(out_shape),
+        out_shape=out_shape,
+        scratch_shapes=scratch,
+        compiler_params=pltpu.CompilerParams(
+            collective_id=collective_id, has_side_effects=True, vmem_limit_bytes=60 << 20
+        ),
+        name="fast_reduce",
+    )(*blocks)
+
+
+PLANE = 4
+CHIP = 2
+LINE = 4
+
+
+def small_plane():
+    return lax.axis_size("rep") == PLANE and lax.axis_size("fsdp") == CHIP * LINE
 
 
 def gather(block):
     return lax.all_gather(block, "fsdp", axis=0, tiled=True)
+
+
+def gather_all(blocks, by_rows, collective_id):
+    if small_plane():
+        return fast_gather(blocks, LINE, by_rows, collective_id)
+    return [gather(block) for block in blocks]
 
 
 def scatter(block):
@@ -439,6 +1107,16 @@
         outs.append(own[:, start : start + size].astype(F32))
         start += size
     return outs
+
+
+def scatter_last(groups, vector, collective_id):
+    if small_plane():
+        *outs, total = fast_reduce(
+            groups, ["four"] * len(groups), LINE, collective_id, vector
+        )
+        return [[out[index] for index in range(4)] for out in outs], total
+    outs = [scatter_columns([scatter(item) for item in group]) for group in groups]
+    return outs, lax.psum(vector, ("rep", "fsdp"))
 
 
 def body(
@@ -467,20 +1145,21 @@
     shard = gain_self.shape[0]
     groups = width // shard
     entries = rel_bias.shape[0]
+    ffn = gate_weight.shape[1]
     small = jnp.stack(
         [gain_self, gain_cross, gain_feed, jnp.pad(rel_bias, (0, shard - entries))], axis=1
     )
-    small = jnp.pad(small, ((0, 0), (0, LANES - 4)))
-    first = gather(
-        jnp.concatenate([interleave(self_query, self_key, self_value), small], axis=1)
-    )
-    second = gather(
-        jnp.concatenate(
-            [self_out, cross_query, interleave(cross_key, cross_value), cross_out], axis=1
-        )
-    )
+    small = jnp.pad(small, ((0, 0), (0, 2 * LANES - 4)))
     gate_up = gather(jnp.concatenate([gate_weight, up_weight], axis=1))
     down = gather(down_weight)
+    (first,) = gather_all(
+        [jnp.concatenate([self_query, self_key, self_value, small], axis=1)], [False], 1
+    )
+    second_own = jnp.concatenate(
+        [self_out, cross_query, cross_key, cross_value, cross_out, small], axis=1
+    )
+    second_own, first = lax.optimization_barrier((second_own, first))
+    (second,) = gather_all([second_own], [False], 2)
     qkv_proj = first[:, : 3 * width]
     vectors = first[:, 3 * width : 3 * width + 4].T
     gain_first = vectors[0:1].astype(F32)
@@ -490,8 +1169,7 @@
     out_self = second[:, :width]
     query_cross = second[:, width : 2 * width]
     kv_cross = second[:, 2 * width : 4 * width]
-    out_cross = second[:, 4 * width :]
-    ffn = gate_weight.shape[1]
+    out_cross = second[:, 4 * width : 5 * width]
     gate_proj = gate_up[:, :ffn]
     up_proj = gate_up[:, ffn:]
 
@@ -521,48 +1199,49 @@
     hidden = (gelu_tanh(gate_pre) * up_pre).astype(BF16)
     result = (later + matmul(hidden, down)).astype(BF16)
 
-    down_own = scatter(weight_term(hidden, upstream))
+    down_term = weight_term(hidden, upstream).astype(BF16)
     hidden_grad = back_term(upstream, down)
     gate_grad = (hidden_grad * up_pre * gelu_slope(gate_pre)).astype(BF16)
     lift_grad = (hidden_grad * gelu_tanh(gate_pre)).astype(BF16)
-    feed_own = scatter(
-        jnp.concatenate(
-            [
-                weight_term(normed_third, gate_grad).astype(BF16),
-                weight_term(normed_third, lift_grad).astype(BF16),
-            ],
-            axis=1,
-        )
-    )
+    gate_term = weight_term(normed_third, gate_grad).astype(BF16)
+    up_term = weight_term(normed_third, lift_grad).astype(BF16)
+    gate_grad, lift_grad, down_term, gate_term, up_term = lax.optimization_barrier(
+        (gate_grad, lift_grad, down_term, gate_term, up_term)
+    )
+    down_own = scatter(down_term)
+    gate_own = scatter(gate_term)
+    up_own = scatter(up_term)
     third_grad = back_term(gate_grad, gate_proj) + back_term(lift_grad, up_proj)
     carry, gain_third_grad = norm_back(later, scale_third, gain_third, third_grad)
     later_grad = upstream.astype(F32) + carry
     branch_two = later_grad.astype(BF16)
     context_two_grad = back_term(branch_two, out_cross).astype(BF16)
-    query_two_grad, kv_two_grad = run_cross_backward(
+    query_two_grad, key_two_grad, value_two_grad = run_cross_backward(
         query_two, kv_two, context_two_grad, context_two, lse_cross, nseq
     )
-    cross_own = scatter(
-        jnp.concatenate(
-            [
-                weight_term(normed_second, query_two_grad).astype(BF16),
-                weight_term(memory_rows, kv_two_grad).astype(BF16),
-                weight_term(context_two, branch_two).astype(BF16),
-            ],
-            axis=1,
-        )
-    )
-    memory_grad = back_term(kv_two_grad, kv_cross)
+    cross_terms = [
+        weight_term(normed_second, query_two_grad).astype(BF16),
+        weight_term(memory_rows, key_two_grad).astype(BF16),
+        weight_term(memory_rows, value_two_grad).astype(BF16),
+        weight_term(context_two, branch_two).astype(BF16),
+    ]
+    memory_grad = back_term(key_two_grad, kv_cross[:, :width]) + back_term(
+        value_two_grad, kv_cross[:, width:]
+    )
     carry, gain_second_grad = norm_back(
         middle, scale_second, gain_second, back_term(query_two_grad, query_cross)
     )
     middle_grad = later_grad + carry
     branch_one = middle_grad.astype(BF16)
     context_grad = back_term(branch_one, out_self).astype(BF16)
-    qkv_grad, diagonal = run_self_backward(
+    query_grad, key_grad, value_grad, diagonal = run_self_backward(
         prefix_len, qkv, context_grad, context, lse_self, bias, nseq
     )
-    first_grad = back_term(qkv_grad, qkv_proj)
+    first_grad = (
+        back_term(query_grad, qkv_proj[:, :width])
+        + back_term(key_grad, qkv_proj[:, width : 2 * width])
+        + back_term(value_grad, qkv_proj[:, 2 * width :])
+    )
     carry, gain_first_grad = norm_back(start_rows, scale_first, gain_first, first_grad)
     tokens_grad = middle_grad + carry
 
@@ -578,54 +1257,34 @@
     ).reshape(width)
     vector_block = jnp.pad(
         jnp.stack([gain_first_grad, gain_second_grad, gain_third_grad, bias_rows], axis=0),
-        ((0, LANES - 4), (0, 0)),
-    ).T
-    self_own = scatter(
-        jnp.concatenate(
-            [
-                weight_term(normed_first, qkv_grad).astype(BF16),
-                weight_term(context, branch_one).astype(BF16),
-                vector_block.astype(BF16),
-            ],
-            axis=1,
-        )
-    )
-
+        ((0, 4), (0, 0)),
+    )
+    self_terms = [
+        weight_term(normed_first, query_grad).astype(BF16),
+        weight_term(normed_first, key_grad).astype(BF16),
+        weight_term(normed_first, value_grad).astype(BF16),
+        weight_term(context, branch_one).astype(BF16),
+    ]
+    (cross_out_grads, self_out_grads), totals = scatter_last(
+        [cross_terms, self_terms], vector_block, 3
+    )
+    own = lax.dynamic_slice(
+        totals, (0, lax.axis_index("fsdp") * shard), (totals.shape[0], shard)
+    )
     (down_weight_grad,) = scatter_columns([down_own])
-    key_own, value_own = deinterleave(cross_own[:, width : 3 * width], 2)
-    gate_g, up_g, cq_g, ck_g, cv_g, co_g = scatter_columns(
-        [
-            feed_own[:, :ffn],
-            feed_own[:, ffn:],
-            cross_own[:, :width],
-            key_own,
-            value_own,
-            cross_own[:, 3 * width :],
-        ]
-    )
-    q_own, k_own, v_own = deinterleave(self_own[:, : 3 * width], 3)
-    copies = jnp.tile(self_own[:, 4 * width :], (1, lax.axis_size("rep")))
-    sq_g, sk_g, sv_g, so_g, vec = scatter_columns(
-        [q_own, k_own, v_own, self_own[:, 3 * width : 4 * width], copies]
-    )
+    gate_weight_grad, up_weight_grad = scatter_columns([gate_own, up_own])
     return (
         result.reshape(tokens.shape),
         tokens_grad.reshape(tokens.shape),
         memory_grad.reshape(memory.shape),
-        vec[:entries, 3],
-        vec[:, 0],
-        sq_g,
-        sk_g,
-        sv_g,
-        so_g,
-        vec[:, 1],
-        cq_g,
-        ck_g,
-        cv_g,
-        co_g,
-        vec[:, 2],
-        gate_g,
-        up_g,
+        own[3, :entries],
+        own[0],
+        *self_out_grads,
+        own[1],
+        *cross_out_grads,
+        own[2],
+        gate_weight_grad,
+        up_weight_grad,
         down_weight_grad,
     )
 

time: 686 us -> 565 us (0.82)
  waiting for transfers between devices: 212 us -> 24.2 us
  Pallas kernels: 122 us -> 301 us
  local copies, waits for them, and re-layouts: 145 us -> 31.8 us
  matrix products: 145 us -> 166 us
  other arithmetic: 35.6 us -> 20.7 us
    pallas_call x0 -> x3, Pallas kernels: none -> 177 us  [the longest x2 110 us: fast_gather(): pl.pallas_call(functools.partial(gather_kernel, shapes, line), in_specs=[...]
    reduce_scatter x3, waiting for transfers between devices: 77.8 us -> 0.02 us  [scatter(): lax.psum_scatter(block.astype(BF16), 'fsdp', scatter_dimension=0, tiled=T...]
    unnamed x146 -> x96, local copies, waits for them, and re-layouts: 95.3 us -> 20.3 us
    unnamed x14 -> x8, waiting for transfers between devices: 54.9 us -> 0.8 us
    all_gather x4 -> x2, waiting for transfers between devices: 52.6 us -> 0.01 us  [gather(): return lax.all_gather(block, 'fsdp', axis=0, tiled=True)]
    slice x20 -> x0, local copies, waits for them, and re-layouts: 25.1 us -> none  [the longest x5 8.6 us: deinterleave(): split[:, :, index].reshape(rows, PAIRS * LANES)]
    dot_general x8 -> x11, matrix products: 54.2 us -> 76.7 us  [back_term(): lax.dot_general(gradient, weight, LAST_DIMS, preferred_element_type=F32)]
    dot_general x8, matrix products: 53.8 us -> 42.6 us  [matmul(): return jnp.dot(left_side, right_side, preferred_element_type=F32)]
  transfers between devices with their start and end apart: 11 -> 7, of which waited for: 8 -> 1; matrix products, arithmetic and copies ran while one was open for 39% -> 30% of each run, Pallas kernels for 13% -> 54%
where the time goes in v2:
time: 565 us; the launch traced here: 559 us
  Pallas kernels  301 us (53%)
  matrix products  166 us (29%)
  local copies, waits for them, and re-layouts  31.8 us (6%)
  waiting for transfers between devices  24.2 us (4%)
  other arithmetic  20.7 us (4%)
  between operations  14.8 us (3%)
    pallas_call x2, Pallas kernels, fast_gather(): pl.pallas_call(functools.partial(gather_kernel, shapes, line), in_specs=[...  110 us
    dot_general x11, matrix products, back_term(): lax.dot_general(gradient, weight, LAST_DIMS, preferred_element_type=F32)  76.7 us
    pallas_call x1, Pallas kernels, fast_reduce(): pl.pallas_call(functools.partial(reduce_kernel, shapes, line, 0 if vector...  66.6 us
    dot_general x11, matrix products, weight_term(): lax.dot_general(inputs, gradient, FIRST_DIMS, preferred_element_type=F32)  46.1 us
    dot_general x8, matrix products, matmul(): return jnp.dot(left_side, right_side, preferred_element_type=F32)  42.6 us
    pallas_call x1, Pallas kernels, run_cross_backward(): pl.pallas_call(cross_backward, grid=(nseq, PAIRS), in_specs=[rows, wide,...  36.1 us
    pallas_call x1, Pallas kernels, run_self_backward(): pl.pallas_call(self_backward, grid_spec=pltpu.PrefetchScalarGridSpec(num_...  34.8 us
    pallas_call x1, Pallas kernels, run_cross_forward(): pl.pallas_call(cross_forward, grid=(nseq, PAIRS), in_specs=[spec((length,...  24.9 us
  transfers between devices with their start and end apart: 7, of which 1 were waited for; matrix products, arithmetic and copies ran while one was open for 30% of the time, Pallas kernels for 54%

profile of v2, /device:TPU:0, one launch (start us, length us, event | category | flops | bytes accessed | tf_op | source)
XLA Modules:
  0.0 558.9 jit_solution(9424377543930351532)
XLA Ops:
  20.5 53.1 %fast_gather.2 = bf16[768,2560]{1,0:T(8,128)(2,1)} custom-call(bf16[96,2560]{1,0:T(8,128)(2,1)} %pad_maximum_fusion.2.refs_0_), custom_call_target="tpu_custom_call" | custom-call | tf_op jit(solution)/shard_map/fast_gather/pallas_call | solution.py:672
  79.3 5.4 convolution_convert_fusion.1.query_ref.key_ref.value_ref
  85.0 57.3 %fast_gather.3 = bf16[768,4096]{1,0:T(8,128)(2,1)} custom-call(bf16[96,4096]{1,0:T(8,128)(2,1)} %get-tuple-element.41.refs_0_), custom_call_target="tpu_custom_call" | custom-call | tf_op jit(solution)/shard_map/fast_gather/pallas_call | solution.py:672
  143.5 4.9 skewed_bias.1.bias_ref
  148.4 23.1 %self_forward.1 = (bf16[1024,768]{1,0:T(8,128)(2,1)}, f32[2,6,2,512]{3,2,1,0:T(2,128)}) custom-call(s32[2]{0:T(128)} %prefix_ref.3, bf16[1024,2304]{1,0:T(8,128)(2,1)} %convolution_convert_fusion.1.query_ref.key_ref.value_ref, bf16[1024,2304]{1,0:T(8,128)(2,1)} %convolution_convert_fusion.1.query_ref.key_ref.value_ref, ...), custom_call_target="tpu_custom_call" | custom-call | flops 20000000000 | bytes 12000000 | tf_op jit(solution)/shard_map/self_forward/pallas_call | solution.py:310
  171.5 3.9 multiply_reduce_fusion.5
  178.2 6.9 %fusion.7.key_ref.value_ref = bf16[2048,1536]{1,0:T(8,128)(2,1)} fusion(bf16[2048,768]{1,0:T(8,128)(2,1)S(1)} %bitcast.116, bf16[768,4096]{1,0:T(8,128)(2,1)S(1)} %copy-done.13), kind=kOutput, calls=%fused_computation.13 | convolution fusion | flops 4834983936 | bytes 11796480 | tf_op jit(solution)/shard_map/dot_general | solution.py:29
  185.2 24.9 %cross_forward.1 = (bf16[1024,768]{1,0:T(8,128)(2,1)}, f32[2,6,2,512]{3,2,1,0:T(2,128)}) custom-call(bf16[1024,768]{1,0:T(8,128)(2,1)} %convolution_convert_fusion.7.query_ref, bf16[2048,1536]{1,0:T(8,128)(2,1)} %fusion.7.key_ref.value_ref, bf16[2048,1536]{1,0:T(8,128)(2,1)} %fusion.7.key_ref.value_ref), custom_call_target="tpu_custom_call" | custom-call | flops 24000000000 | bytes 10000000 | tf_op jit(solution)/shard_map/cross_forward/pallas_call | solution.py:340
  210.0 4.2 multiply_reduce_fusion.4
  217.4 9.2 %fusion.22 = f32[1024,2048]{1,0:T(8,128)} fusion(bf16[1024,768]{1,0:T(8,128)(2,1)} %multiply_convert_fusion.2, bf16[768,4096]{1,0:T(8,128)(2,1)} %all-gather.3.cloned.1.call-done), kind=kOutput, calls=%fused_computation.50 | convolution fusion | flops 3221225472 | bytes 13107200 | tf_op jit(solution)/shard_map/dot_general | solution.py:29
  226.5 5.8 %fusion.26 = f32[1024,2048]{1,0:T(8,128)} fusion(bf16[1024,768]{1,0:T(8,128)(2,1)S(1)} %copy-done.17, bf16[768,4096]{1,0:T(8,128)(2,1)S(1)} %copy-done.31), kind=kOutput, calls=%fused_computation.54 | convolution fusion | flops 3221225472 | bytes 13107200 | tf_op jit(solution)/shard_map/dot_general | solution.py:29
  232.3 16.5 %multiply_convert_fusion = (bf16[1024,2048]{1,0:T(8,128)(2,1)S(1)}, bf16[1024,2048]{1,0:T(8,128)(2,1)}, bf16[1024,2048]{1,0:T(8,128)(2,1)}) fusion(f32[1024,2048]{1,0:T(8,128)} %fusion.26, f32[1024,2048]{1,0:T(8,128)} %fusion.22, bf16[1024,768]{1,0:T(8,128)(2,1)} %bitcast.123, bf16[2048,768]{1,0:T(8,128)(2,1)} %all-gather.5.cloned.1.call-done), kind=kOutput, calls=%fused_computation.9 | convolution fusion | flops 3273654272 | bytes 34078720 | tf_op jit(solution)/shard_map/dot_general | solution.py:37
  250.8 5.1 convolution_convert_fusion.2
  255.9 8.0 %convolution_convert_fusion.3 = bf16[768,2048]{1,0:T(8,128)(2,1)} fusion(bf16[1024,768]{1,0:T(8,128)(2,1)} %multiply_convert_fusion.2, bf16[1024,2048]{1,0:T(8,128)(2,1)} %get-tuple-element.43), kind=kOutput, calls=%fused_computation.18 | convolution fusion | flops 3222798336 | bytes 8912896 | tf_op jit(solution)/shard_map/dot_general | solution.py:33
  263.9 8.0 %convolution_convert_fusion.4 = bf16[2048,768]{1,0:T(8,128)(2,1)} fusion(bf16[1024,2048]{1,0:T(8,128)(2,1)} %get-tuple-element.125, bf16[1024,768]{1,0:T(8,128)(2,1)} %bitcast.124), kind=kOutput, calls=%fused_computation.19 | convolution fusion | flops 3222798336 | bytes 8912896 | tf_op jit(solution)/shard_map/dot_general | solution.py:33
  272.0 6.9 %fusion.20 = f32[1024,768]{1,0:T(8,128)S(1)} fusion(bf16[1024,2048]{1,0:T(8,128)(2,1)} %copy-done.36, bf16[768,4096]{1,0:T(8,128)(2,1)} %all-gather.3.cloned.1.call-done), kind=kOutput, calls=%fused_computation.48 | convolution fusion | flops 3221225472 | bytes 10485760 | tf_op jit(solution)/shard_map/dot_general | solution.py:37
  278.9 5.9 %multiply_reduce_fusion = (f32[768]{0:T(1024)S(1)}, f32[1024]{0:T(1024)S(1)}, f32[1024,768]{1,0:T(8,128)S(1)}) fusion(f32[1024,768]{1,0:T(8,128)S(1)} %copy-done.2, f32[1024]{0:T(1024)S(1)} %add_rsqrt_fusion, f32[768]{0:T(1024)S(1)} %get-tuple-element.120, f32[1024,768]{1,0:T(8,128)S(1)} %fusion.20, bf16[1024,2048]{1,0:T(8,128)(2,1)S(1)} %copy-done.35, ...), kind=kOutput, calls=%fused_computation.36 | convolution fusion | flops 3226728704 | bytes 16791552 | tf_op jit(solution)/shard_map/dot_general | solution.py:37
  291.6 36.1 %cross_backward.1 = (bf16[1024,768]{1,0:T(8,128)(2,1)}, bf16[2048,768]{1,0:T(8,128)(2,1)}, bf16[2048,768]{1,0:T(8,128)(2,1)}) custom-call(bf16[1024,768]{1,0:T(8,128)(2,1)} %convolution_convert_fusion.7.query_ref, bf16[2048,1536]{1,0:T(8,128)(2,1)} %fusion.7.key_ref.value_ref, bf16[2048,1536]{1,0:T(8,128)(2,1)} %fusion.7.key_ref.value_ref, ...), custom_call_target="tpu_custom_call" | custom-call | flops 35999997952 | bytes 20000000 | tf_op jit(solution)/shard_map/cross_backward/pallas_call | solution.py:368
  327.8 4.7 multiply_reduce_fusion.1
  333.4 4.8 convolution_convert_fusion.5.up_ref
  338.2 34.8 %self_backward.1 = (bf16[1024,768]{1,0:T(8,128)(2,1)}, bf16[1024,768]{1,0:T(8,128)(2,1)}, bf16[1024,768]{1,0:T(8,128)(2,1)}, f32[6,2,1024]{2,1,0:T(2,128)}) custom-call(s32[2]{0:T(128)} %prefix_ref.3, bf16[1024,2304]{1,0:T(8,128)(2,1)} %convolution_convert_fusion.1.query_ref.key_ref.value_ref, ...), custom_call_target="tpu_custom_call" | custom-call | flops 24000000000 | bytes 20000000 | tf_op jit(solution)/shard_map/self_backward/pallas_call | solution.py:395
  373.0 4.9 fusion.38
  378.0 4.4 fusion.40
  383.0 7.7 %fusion.19 = (f32[768]{0:T(1024)S(1)}, f32[1024]{0:T(1024)S(1)}, f32[1024,768]{1,0:T(8,128)}) fusion(bf16[2,512,768]{2,1,0:T(8,128)(2,1)} %param.20, f32[1024]{0:T(1024)S(1)} %bitcast.127, f32[768]{0:T(1024)S(1)} %copy-done.25, bf16[1024,768]{1,0:T(8,128)(2,1)} %get-tuple-element.50, bf16[768,2560]{1,0:T(8,128)(2,1)} %fast_gather.2, ...), kind=kOutput, calls=%fused_computation.35 | convolution fusion | flops 1215035648 | bytes 13776896 | tf_op jit(solution)/shard_map/dot_general | solution.py:37
  392.2 4.5 convolution_convert_fusion.10.refs_5_
  409.5 4.1 fusion.32.refs_1_
  417.3 66.6 %fast_reduce.1 = (f32[4,96,192]{2,1,0:T(8,128)}, f32[4,96,192]{2,1,0:T(8,128)}, f32[8,768]{1,0:T(8,128)}) custom-call(bf16[768,768]{1,0:T(8,128)(2,1)} %convolution_convert_fusion.15.refs_0_, bf16[768,768]{1,0:T(8,128)(2,1)} %fusion.32.refs_1_, bf16[768,768]{1,0:T(8,128)(2,1)} %fusion.33.refs_2_, bf16[768,768]{1,0:T(8,128)(2,1)} %convolution_convert_fusion.12.refs_3_, ...), custom_call_target="tpu_custom_call" | custom-call | tf_op jit(solution)/shard_map/fast_reduce/pallas_call | solution.py:1061
  487.3 7.6 %fusion.35 = f32[2048,768]{1,0:T(8,128)} fusion(bf16[2048,768]{1,0:T(8,128)(2,1)} %get-tuple-element.51, bf16[768,4096]{1,0:T(8,128)(2,1)} %fast_gather.3), kind=kOutput, calls=%fused_computation.73 | convolution fusion | flops 2415919104 | bytes 10616832 | tf_op jit(solution)/shard_map/dot_general | solution.py:37
  497.0 9.5 %convolution_add_fusion = f32[2048,768]{1,0:T(8,128)} fusion(f32[2048,768]{1,0:T(8,128)} %fusion.35, bf16[2048,768]{1,0:T(8,128)(2,1)} %get-tuple-element.52, bf16[768,4096]{1,0:T(8,128)(2,1)} %fast_gather.3), kind=kOutput, calls=%fused_computation.16 | convolution fusion | flops 2417491968 | bytes 16908288 | tf_op jit(solution)/shard_map/dot_general | solution.py:37
  512.9 6.1 %fusion.15 = f32[1024,768]{1,0:T(8,128)} fusion(f32[1024,768]{1,0:T(8,128)} %copy-done.8, bf16[2,512,768]{2,1,0:T(8,128)(2,1)} %param.20, f32[1024,768]{1,0:T(8,128)} %get-tuple-element.147, f32[1024]{0:T(1024)S(1)} %broadcast_multiply_fusion, f32[768]{0:T(1024)S(1)} %copy-done.25, f32[1024]{0:T(1024)S(1)} %bitcast.128), kind=kLoop, calls=%fused_computation.31 | loop fusion | flops 7077888 | bytes 11021312 | tf_op jit(solution)/shard_map/add | solution.py:1246
  520.5 4.5 add_convert_fusion
  526.8 23.4 %reduce-scatter.12.cloned.1.call-done = bf16[96,1024]{1,0:T(8,128)(2,1)} async-done(((bf16[96,4096]{1,0:T(8,128)(2,1)}), bf16[96,1024]{1,0:T(8,128)(2,1)}) %reduce-scatter.12.cloned.1.call-update) | async-done | bytes 196624 | tf_op jit(solution)/shard_map/reduce_scatter | solution.py:1102
  (166 shorter events, 71.5 us)
Async XLA Ops:
  7.2 171.0 %copy-start = (bf16[2,1024,768]{2,1,0:T(8,128)(2,1)S(1)}, bf16[2,1024,768]{2,1,0:T(8,128)(2,1)}, u32[]{:S(2)}) copy-start(bf16[2,1024,768]{2,1,0:T(8,128)(2,1)} %param.21) | copy-start | bytes 9437188
  7.2 6.2 %copy-start.22 = (bf16[96,768]{1,0:T(8,128)(2,1)S(1)}, bf16[96,768]{1,0:T(8,128)(2,1)}, u32[]{:S(2)}) copy-start(bf16[96,768]{1,0:T(8,128)(2,1)} %param.31) | copy-start | bytes 442372
  7.2 6.9 %copy-start.23 = (bf16[96,768]{1,0:T(8,128)(2,1)S(1)}, bf16[96,768]{1,0:T(8,128)(2,1)}, u32[]{:S(2)}) copy-start(bf16[96,768]{1,0:T(8,128)(2,1)} %param.32) | copy-start | bytes 442372
  7.2 210.1 %all-gather.3.cloned.1.call-start = ((), (), s32[]{:S(2)}) async-start(), calls=%async_computation.5 | async-start | bytes 7077888 | tf_op jit(solution)/shard_map/all_gather | solution.py:1084
  9.5 222.8 %all-gather.5.cloned.1.call-start = ((), (), s32[]{:S(2)}) async-start(), calls=%async_computation.6 | async-start | bytes 3538944 | tf_op jit(solution)/shard_map/all_gather | solution.py:1084
  10.3 484.5 %reduce-scatter.14.cloned.1.call-start = ((), (), s32[]{:S(2)}) async-start(), calls=%async_computation.10 | async-start | bytes 3538944 | tf_op jit(solution)/shard_map/reduce_scatter | solution.py:1094
  73.6 4.2 copy-start.4
  73.6 5.7 %copy-start.14 = (bf16[768,2560]{1,0:T(8,128)(2,1)S(1)}, bf16[768,2560]{1,0:T(8,128)(2,1)}, u32[]{:S(2)}) copy-start(bf16[768,2560]{1,0:T(8,128)(2,1)} %fast_gather.2) | copy-start | bytes 11796484
  79.3 5.6 copy-start.30
  171.5 4.1 copy-start.13
  217.4 9.2 %copy-start.17 = (bf16[1024,768]{1,0:T(8,128)(2,1)S(1)}, bf16[1024,768]{1,0:T(8,128)(2,1)}, u32[]{:S(2)}) copy-start(bf16[1024,768]{1,0:T(8,128)(2,1)} %multiply_convert_fusion.2) | copy-start | bytes 4718596
  217.4 9.2 %copy-start.31 = (bf16[768,4096]{1,0:T(8,128)(2,1)S(1)}, bf16[768,4096]{1,0:T(8,128)(2,1)}, u32[]{:S(2)}) copy-start(bf16[768,4096]{1,0:T(8,128)(2,1)} %all-gather.3.cloned.1.call-done) | copy-start | bytes 18874372
  232.3 18.5 %copy-start.18 = (bf16[1024,768]{1,0:T(8,128)(2,1)S(1)}, bf16[1024,768]{1,0:T(8,128)(2,1)}, u32[]{:S(2)}) copy-start(bf16[1024,768]{1,0:T(8,128)(2,1)} %multiply_convert_fusion.2) | copy-start | bytes 4718596
  271.9 234.6 %reduce-scatter.8.cloned.1.call-start = ((), (), s32[]{:S(2)}) async-start(), calls=%async_computation.7 | async-start | bytes 3538944 | tf_op jit(solution)/shard_map/reduce_scatter | solution.py:1094
  272.0 7.0 %copy-start.2 = (f32[1024,768]{1,0:T(8,128)S(1)}, f32[1024,768]{1,0:T(8,128)}, u32[]{:S(2)}) copy-start(f32[1024,768]{1,0:T(8,128)} %copy-done.1) | copy-start | bytes 9437188
  272.0 7.0 %copy-start.35 = (bf16[1024,2048]{1,0:T(8,128)(2,1)S(1)}, bf16[1024,2048]{1,0:T(8,128)(2,1)}, u32[]{:S(2)}) copy-start(bf16[1024,2048]{1,0:T(8,128)(2,1)} %get-tuple-element.43) | copy-start | bytes 12582916
  278.9 5.9 %copy-start.19 = (bf16[2,512,768]{2,1,0:T(8,128)(2,1)S(1)}, bf16[2,512,768]{2,1,0:T(8,128)(2,1)}, u32[]{:S(2)}) copy-start(bf16[2,512,768]{2,1,0:T(8,128)(2,1)} %param.39) | copy-start | bytes 4718596
  291.6 216.2 %reduce-scatter.10.cloned.1.call-start = ((), (), s32[]{:S(2)}) async-start(), calls=%async_computation.8 | async-start | bytes 3538944 | tf_op jit(solution)/shard_map/reduce_scatter | solution.py:1094
  327.7 4.7 copy-start.6
  327.7 4.7 copy-start.11
  333.4 4.8 copy-start.8
  373.0 5.0 copy-start.37
  382.4 142.6 %reduce-scatter.16.cloned.1.call-start = ((), (), s32[]{:S(2)}) async-start(), calls=%async_computation.11 | async-start | bytes 491520
  383.0 7.7 %copy-start.28 = (f32[6,2,1024]{2,1,0:T(2,128)S(1)}, f32[6,2,1024]{2,1,0:T(2,128)}, u32[]{:S(2)}) copy-start(f32[6,2,1024]{2,1,0:T(2,128)} %get-tuple-element.53) | copy-start | bytes 147460
  383.0 7.7 %copy-start.29 = (s32[1024]{0:T(1024)S(1)}, s32[1024]{0:T(1024)}, u32[]{:S(2)}) copy-start(s32[1024]{0:T(1024)} %pad.27) | copy-start | bytes 12292
  392.2 4.5 copy-start.16
  392.2 4.5 copy-start.38
  409.5 4.1 copy-start.34
  496.8 53.4 %reduce-scatter.12.cloned.1.call-start = ((), (), s32[]{:S(2)}) async-start(), calls=%async_computation.9 | async-start | bytes 983040 | tf_op jit(solution)/shard_map/reduce_scatter | solution.py:1102
  512.9 6.1 %copy-start.3 = (f32[1024,768]{1,0:T(8,128)S(1)}, f32[1024,768]{1,0:T(8,128)}, u32[]{:S(2)}) copy-start(f32[1024,768]{1,0:T(8,128)} %copy-done.1) | copy-start | bytes 9437188
  512.9 6.1 %copy-start.32 = (bf16[2048,768]{1,0:T(8,128)(2,1)S(1)}, bf16[2048,768]{1,0:T(8,128)(2,1)}, u32[]{:S(2)}) copy-start(bf16[2048,768]{1,0:T(8,128)(2,1)} %all-gather.5.cloned.1.call-done) | copy-start | bytes 9437188
  512.9 7.6 %copy-start.41 = (bf16[1024,2048]{1,0:T(8,128)(2,1)S(1)}, bf16[1024,2048]{1,0:T(8,128)(2,1)}, u32[]{:S(2)}) copy-start(bf16[1024,2048]{1,0:T(8,128)(2,1)} %get-tuple-element.125) | copy-start | bytes 12582916
  (17 other events, 33.7 us)
Sparse Core Ops, SparseCore 0:
  9.7 73.5 all-gather.2
  84.9 44.8 all-gather.4
  272.0 40.0 reduce-scatter.13
  314.3 39.7 reduce-scatter.7
  382.5 40.1 reduce-scatter.9
  496.9 24.1 reduce-scatter.15
  524.0 26.1 reduce-scatter.11
